TPU v7x, 1024 devices: a whole 4x8x16 slice. The times are simulated.
1024 devices in a mesh: gx: 16 (over y, core), gy: 4 (over x), gz: 16 (over z).
Axes of the slice: x: 4, y: 8, z: 16, core: 2. Of those that a mesh axis runs over, the one named last changes fastest.
Arguments:
- old_basis: float32 [4, 128, 64, 2048], P(None, 'gx', 'gy', 'gz'), may hold values from -4 to 4, as said below
- previous: float32 [4, 128, 64, 2048], P(None, 'gx', 'gy', 'gz'), as said below
- incoming: float32 [4, 128, 64, 2048], P(None, 'gx', 'gy', 'gz'), may hold values from -6 to 6
- coefficient: float32 [128, 64, 2048], P('gx', 'gy', 'gz'), may hold values from 0.5 to 4
Outputs:
- orthonormal: float32 [4, 128, 64, 2048], P(None, 'gx', 'gy', 'gz')
- projection: float32 [4, 4], replicated
- triangle: float32 [4, 4], replicated
- preconditioned: float32 [4, 128, 64, 2048], P(None, 'gx', 'gy', 'gz')
- operated: float32 [4, 128, 64, 2048], P(None, 'gx', 'gy', 'gz')
Inputs may be any that keep to these rules, and one draw needn't show every extreme that they name: `old_basis`: entries of order one; the basis vectors are independent, so every Gram matrix formed from them is well conditioned. `previous`: entries of order one; each vector has a part outside the span of old_basis of norm of order one under the inner product.
All inputs are finite; a program needn't handle non-finite values.
Results may differ from a plain program's by a relative error of at most 0.0003.
Values sent between devices are 32-bit elements; how exact they have to be, the bound alone decides.
A program may use at most 64 MiB of HBM per device.

v0:
```python
import functools

import jax
import jax.numpy as jnp
from jax import lax
from jax.sharding import Mesh
from jax.sharding import PartitionSpec as P

LEVELS = 6
COARSE_SWEEPS = 4
GX_GY_GZ = ("gx_0", "gx_1", "gy", "gz")
GX = ("gx_0", "gx_1")


OMEGA = 0.8
HIGH = lax.Precision.HIGHEST


def extended_2(shard, sides, width):
    edges = {}
    for axis, dim in sides:
        count, length = (lax.axis_size(axis), shard.shape[dim])
        up = [(i, (i + 1) % count) for i in range(count - 1)]
        last = lax.slice_in_dim(shard, length - width, length, axis=dim)
        leading = lax.slice_in_dim(shard, 0, width, axis=dim)
        edges[dim] = (
            lax.ppermute(last, axis, up),
            lax.ppermute(leading, axis, [(b, a) for a, b in up]),
        )
    done = []
    for _, dim in sides:
        low, high = edges[dim]
        around = [(width, width) if d in done else (0, 0) for d in range(shard.ndim)]
        shard = jnp.concatenate([jnp.pad(low, around), shard, jnp.pad(high, around)], axis=dim)
        done.append(dim)
    return shard


def laid_out(pieces, dim):
    pieces = jnp.moveaxis(pieces, 0, dim)
    shape = pieces.shape
    return pieces.reshape(*shape[:dim], shape[dim] * shape[dim + 1], *shape[dim + 2 :])


def gather_in_order(shard, axes, sequence):
    pieces = shard
    for k in sequence:
        pieces = lax.all_gather(pieces, axes[k])
    done = sequence[::-1]
    back = [done.index(k) for k in range(len(axes))]
    pieces = pieces.transpose(*back, *range(len(axes), pieces.ndim))
    return pieces.reshape(-1, *shard.shape)


def gathered_by_axis(shard, axes, sequence, dim):
    return laid_out(gather_in_order(shard, axes, sequence), dim)


def over_axes(shard, axes):
    return functools.reduce(lax.psum, axes, shard)


def stencil(extended, coeffs, factor):
    center = extended[:, 1:-1, 1:-1, 1:-1]
    total = extended[:, 2:, 1:-1, 1:-1] + extended[:, :-2, 1:-1, 1:-1]
    total = total + extended[:, 1:-1, 2:, 1:-1] + extended[:, 1:-1, :-2, 1:-1]
    total = total + extended[:, 1:-1, 1:-1, 2:] + extended[:, 1:-1, 1:-1, :-2]
    return factor * coeffs * (6.0 * center - total)


def zero_margin(field):
    return jnp.pad(field, ((0, 0), (1, 1), (1, 1), (1, 1)))


def with_faces(field):
    return extended_2(field, ((GX, 1), ("gy", 2), ("gz", 3)), 1)


def restrict(field):
    depth, size_a, size_b, size_c = field.shape
    return field.reshape(depth, size_a // 2, 2, size_b // 2, 2, size_c // 2, 2).mean(axis=(2, 4, 6))


def prolong(field):
    return jnp.repeat(jnp.repeat(jnp.repeat(field, 2, axis=1), 2, axis=2), 2, axis=3)


def whole_cycle(source, coeff_list, level):
    coeffs = coeff_list[level]
    factor = 0.25**level
    diagonal = 6.0 * factor * coeffs
    iterate = OMEGA * source / diagonal
    if level == LEVELS - 1:
        for sweep in range(COARSE_SWEEPS - 1):
            iterate = (
                iterate
                + OMEGA * (source - stencil(zero_margin(iterate), coeffs, factor)) / diagonal
            )
        return iterate
    iterate = iterate + OMEGA * (source - stencil(zero_margin(iterate), coeffs, factor)) / diagonal
    residue = source - stencil(zero_margin(iterate), coeffs, factor)
    iterate = iterate + prolong(whole_cycle(restrict(residue), coeff_list, level + 1))
    iterate = iterate + OMEGA * (source - stencil(zero_margin(iterate), coeffs, factor)) / diagonal
    return iterate


def agglomerate(source, coeffs, start_level):
    vectors = source.shape[0]
    stacked = jnp.concatenate([source, coeffs[None]], axis=0)
    depth, size_a, size_b, size_c = stacked.shape
    flattened = stacked.reshape(depth, size_a * size_b * size_c)
    gathered = gathered_by_axis(flattened, GX_GY_GZ, (0, 3, 2, 1), 1)
    count_x, count_y, count_z = (lax.axis_size(GX), lax.axis_size("gy"), lax.axis_size("gz"))
    gathered = gathered.reshape(depth, count_x, count_y, count_z, size_a, size_b, size_c)
    gathered = gathered.transpose(0, 1, 4, 2, 5, 3, 6).reshape(
        depth, count_x * size_a, count_y * size_b, count_z * size_c
    )
    coarse_list = [gathered[vectors]]
    for level in range(LEVELS - 1 - start_level):
        coarse_list.append(restrict(coarse_list[-1][None])[0])
    solution = whole_cycle(gathered[:vectors], [None] * start_level + coarse_list, start_level)
    starts = (
        jnp.zeros((), jnp.int32),
        lax.axis_index(GX) * size_a,
        lax.axis_index("gy") * size_b,
        lax.axis_index("gz") * size_c,
    )
    return lax.dynamic_slice(solution, starts, (vectors, size_a, size_b, size_c))


def local_cycle(source, coeff_list, level, start_level):
    coeffs = coeff_list[level]
    if level == start_level:
        return agglomerate(source, coeffs, start_level)
    factor = 0.25**level
    diagonal = 6.0 * factor * coeffs
    iterate = OMEGA * source / diagonal
    iterate = iterate + OMEGA * (source - stencil(with_faces(iterate), coeffs, factor)) / diagonal
    residue = source - stencil(with_faces(iterate), coeffs, factor)
    iterate = iterate + prolong(local_cycle(restrict(residue), coeff_list, level + 1, start_level))
    iterate = iterate + OMEGA * (source - stencil(with_faces(iterate), coeffs, factor)) / diagonal
    return iterate


def triangular_inverse(lower):
    order = lower.shape[0]
    identity = jnp.eye(order, dtype=lower.dtype)
    inverse = jnp.zeros_like(lower)
    for row in range(order):
        values = identity[row] - jnp.dot(lower[row, :row], inverse[:row], precision=HIGH)
        inverse = inverse.at[row].set(values / lower[row, row])
    return inverse


def per_device(old_basis, previous, incoming, coefficient):
    local_cells = old_basis.shape[1] * old_basis.shape[2] * old_basis.shape[3]
    total_cells = float(local_cells * lax.axis_size(GX) * lax.axis_size("gy") * lax.axis_size("gz"))
    basis_local = jnp.einsum("mxyz,jxyz->mj", old_basis, previous, precision=HIGH)
    self_local = jnp.einsum("ixyz,jxyz->ij", previous, previous, precision=HIGH)
    correlation_local = jnp.einsum("mxyz,nxyz->mn", old_basis, old_basis, precision=HIGH)
    summed = (
        over_axes(basis_local, GX_GY_GZ),
        over_axes(self_local, GX_GY_GZ),
        over_axes(correlation_local, GX_GY_GZ),
    )
    projection = summed[0] / total_cells
    cross = summed[1] / total_cells
    correlation = summed[2] / total_cells
    squared = jnp.dot(projection.T, projection, precision=HIGH)
    weighted = jnp.dot(
        projection.T, jnp.dot(correlation, projection, precision=HIGH), precision=HIGH
    )
    gram = cross - 2.0 * squared + weighted
    remainder = previous - jnp.einsum("mxyz,mj->jxyz", old_basis, projection, precision=HIGH)
    start_level = LEVELS - 3
    coeff_list = [coefficient]
    for level in range(start_level):
        coeff_list.append(restrict(coeff_list[-1][None])[0])
    preconditioned = local_cycle(incoming, coeff_list, 0, start_level)
    operated = stencil(with_faces(preconditioned), coefficient, 1.0)
    lower = jnp.linalg.cholesky(gram)
    inverse = triangular_inverse(lower)
    orthonormal = jnp.einsum("ji,ixyz->jxyz", inverse, remainder, precision=HIGH)
    return (orthonormal, projection, lower.T, preconditioned, operated)


def solution(mesh):
    split = Mesh(
        mesh.devices.reshape(8, 2, mesh.shape["gy"], mesh.shape["gz"]), ("gx_0", "gx_1", "gy", "gz")
    )
    in_specs = (
        P(None, GX, "gy", "gz"),
        P(None, GX, "gy", "gz"),
        P(None, GX, "gy", "gz"),
        P(GX, "gy", "gz"),
    )
    out_specs = (
        P(None, GX, "gy", "gz"),
        P(),
        P(),
        P(None, GX, "gy", "gz"),
        P(None, GX, "gy", "gz"),
    )
    return jax.shard_map(
        per_device, mesh=split, in_specs=in_specs, out_specs=out_specs, check_vma=False
    )
```

profile of v0, /device:TPU:290, one launch (start us, length us, event | category | flops | bytes accessed | tf_op | source)
XLA Modules:
  0.0 482.5 jit_solution(17919949341127433623)
XLA Ops:
  5.0 3.4 collective-permute-start.3
  10.4 4.9 %collective-permute-start = (f32[4,1,16,128]{3,2,1,0:T(8,128)S(1)}, f32[4,1,16,128]{3,2,1,0:T(8,128)S(1)}, u32[]{:S(2)}, u32[]{:S(2)}) collective-permute-start(f32[4,1,16,128]{3,2,1,0:T(8,128)S(1)} %get-tuple-element.143), channel_id=1, source_target_pairs={{64,0},{128,64},{192,128},{256,192},{320,256},{384,320},{448,384},... | collective-permute-start | bytes 98312 | tf_op jit(solution)/shard_map/ppermute | solution.py:28
  23.6 5.6 %reshape_broadcast_in_dim.3 = f32[4,2,8,2,64,2]{5,4,3,2,1,0:T(8,128)} reshape(f32[8,16,128]{2,1,0:T(8,128)S(1)} %copy-done.5) | data formatting | bytes 131072 | tf_op jit(solution)/shard_map/reshape;broadcast_in_dim | solution.py:81
  29.1 14.4 %all-reduce.51 = (f32[4,4]{0,1:T(4,128)S(1)}, f32[4,4]{0,1:T(4,128)S(1)}, f32[4,4]{0,1:T(4,128)S(1)}) all-reduce(f32[4,4]{0,1:T(4,128)S(1)} %convolution_bitcast_fusion.1, f32[4,4]{0,1:T(4,128)S(1)} %convolution_bitcast_fusion.2, f32[4,4]{0,1:T(4,128)S(1)} %convolution_bitcast_fusion), channel_id=1, replica_groups=mesh['gx_0'=8,'gx_1'=2,'gy'=4,'gz'=16] {'gx_0'}, use_global_device_ids=true, to_apply=%region_4.0 | all-reduce | flops 48 | bytes 384 | tf_op jit(solution)/shard_map/psum | solution.py:60
  46.1 8.7 %all-reduce.52 = (f32[4,4]{0,1:T(4,128)S(1)}, f32[4,4]{0,1:T(4,128)S(1)}, f32[4,4]{0,1:T(4,128)S(1)}) all-reduce(f32[4,4]{0,1:T(4,128)S(1)} %get-tuple-element.112, f32[4,4]{0,1:T(4,128)S(1)} %get-tuple-element.113, f32[4,4]{0,1:T(4,128)S(1)} %get-tuple-element.114), channel_id=1, replica_groups=mesh['gx_0'=8,'gx_1'=2,'gy'=4,'gz'=16] {'gy'}, use_global_device_ids=true, to_apply=%region_6.0 | all-reduce | flops 48 | bytes 384 | tf_op jit(solution)/shard_map/psum | solution.py:60
  54.7 36.4 %all-reduce.50 = (f32[4,4]{0,1:T(4,128)S(1)}, f32[4,4]{0,1:T(4,128)S(1)}, f32[4,4]{0,1:T(4,128)S(1)}) all-reduce(f32[4,4]{0,1:T(4,128)S(1)} %get-tuple-element.109, f32[4,4]{0,1:T(4,128)S(1)} %get-tuple-element.110, f32[4,4]{0,1:T(4,128)S(1)} %get-tuple-element.111), channel_id=1, replica_groups=mesh['gx_0'=8,'gx_1'=2,'gy'=4,'gz'=16] {'gz'}, use_global_device_ids=true, to_apply=%region_7.0 | all-reduce | flops 48 | bytes 384 | tf_op jit(solution)/shard_map/psum | solution.py:60
  104.1 6.7 %collective-permute-done.5 = f32[4,8,16,1]{3,2,1,0:T(8,128)S(1)} collective-permute-done((f32[4,8,16,1]{3,2,1,0:T(8,128)S(1)}, f32[4,8,16,1]{3,2,1,0:T(8,128)S(1)}, u32[]{:S(2)}, u32[]{:S(2)}) %collective-permute-start.5) | collective-permute-done | bytes 2080 | tf_op jit(solution)/shard_map/ppermute | solution.py:27
  119.1 4.9 %collective-permute-start.6 = (f32[4,1,16,128]{3,2,1,0:T(8,128)S(1)}, f32[4,1,16,128]{3,2,1,0:T(8,128)S(1)}, u32[]{:S(2)}, u32[]{:S(2)}) collective-permute-start(f32[4,1,16,128]{3,2,1,0:T(8,128)S(1)} %get-tuple-element.137), channel_id=1, source_target_pairs={{64,0},{128,64},{192,128},{256,192},{320,256},{384,320},{448,384},... | collective-permute-start | bytes 98312 | tf_op jit(solution)/shard_map/ppermute | solution.py:28
  125.9 4.1 collective-permute-start.11
  133.3 3.1 collective-permute-done.11
  136.8 4.7 copy.1153
  141.5 8.7 %reduce_sum.111 = f32[4,4,8,64]{0,3,2,1:T(8,128)S(1)} reduce(f32[4,4,2,8,2,64,2]{0,6,5,4,3,2,1:T(2,128)} %bitcast.120, f32[]{:T(128)} %constant.228.clone.1), dimensions={2,4,6}, to_apply=%region_14.0 | reduce | flops 57344 | bytes 294916 | tf_op jit(solution)/shard_map/reduce_sum | solution.py:81
  152.6 3.9 collective-permute-start.14
  158.4 4.9 %collective-permute-start.12 = (f32[4,1,8,64]{3,2,1,0:T(8,128)S(1)}, f32[4,1,8,64]{3,2,1,0:T(8,128)S(1)}, u32[]{:S(2)}, u32[]{:S(2)}) collective-permute-start(f32[4,1,8,64]{3,2,1,0:T(8,128)S(1)} %get-tuple-element.179), channel_id=1, source_target_pairs={{64,0},{128,64},{192,128},{256,192},{320,256},{384,320},{448,384},... | collective-permute-start | bytes 24584 | tf_op jit(solution)/shard_map/ppermute | solution.py:28
  165.8 3.4 collective-permute-start.17
  169.5 3.7 collective-permute-done.17
  175.4 3.9 collective-permute-start.20
  181.2 4.9 %collective-permute-start.18 = (f32[4,1,8,64]{3,2,1,0:T(8,128)S(1)}, f32[4,1,8,64]{3,2,1,0:T(8,128)S(1)}, u32[]{:S(2)}, u32[]{:S(2)}) collective-permute-start(f32[4,1,8,64]{3,2,1,0:T(8,128)S(1)} %get-tuple-element.173), channel_id=1, source_target_pairs={{64,0},{128,64},{192,128},{256,192},{320,256},{384,320},{448,384},... | collective-permute-start | bytes 24584 | tf_op jit(solution)/shard_map/ppermute | solution.py:28
  188.1 3.9 collective-permute-start.23
  198.8 3.9 collective-permute-start.26
  204.7 4.9 %collective-permute-start.24 = (f32[4,1,4,32]{0,3,2,1:T(8,128)S(1)}, f32[4,1,4,32]{0,3,2,1:T(8,128)S(1)}, u32[]{:S(2)}, u32[]{:S(2)}) collective-permute-start(f32[4,1,4,32]{0,3,2,1:T(8,128)S(1)} %get-tuple-element.161), channel_id=1, source_target_pairs={{64,0},{128,64},{192,128},{256,192},{320,256},{384,320},{448,384},... | collective-permute-start | bytes 6152 | tf_op jit(solution)/shard_map/ppermute | solution.py:28
  211.5 3.9 collective-permute-start.29
  220.4 3.9 collective-permute-start.32
  226.2 4.9 %collective-permute-start.30 = (f32[4,1,4,32]{0,3,2,1:T(8,128)S(1)}, f32[4,1,4,32]{0,3,2,1:T(8,128)S(1)}, u32[]{:S(2)}, u32[]{:S(2)}) collective-permute-start(f32[4,1,4,32]{0,3,2,1:T(8,128)S(1)} %get-tuple-element.155), channel_id=1, source_target_pairs={{64,0},{128,64},{192,128},{256,192},{320,256},{384,320},{448,384},... | collective-permute-start | bytes 6152 | tf_op jit(solution)/shard_map/ppermute | solution.py:28
  233.0 3.9 collective-permute-start.35
  240.0 24.7 %all_gather.21 = f32[8,5,32]{2,1,0:T(8,128)S(1)} all-gather(f32[1,5,32]{2,1,0:T(8,128)S(1)} %pad_maximum_fusion.160), channel_id=1, replica_groups=mesh['gx_0'=8,'gx_1'=2,'gy'=4,'gz'=16] {'gx_0'}, dimensions={0}, use_global_device_ids=true | all-gather | bytes 5760 | tf_op jit(solution)/shard_map/all_gather | solution.py:48
  264.7 28.4 %all-gather = f32[128,5,32]{2,0,1:T(8,128)S(1)} all-gather(f32[8,5,32]{2,0,1:T(8,128)S(1)} %copy.1161), channel_id=2, replica_groups=mesh['gx_0'=8,'gx_1'=2,'gy'=4,'gz'=16] {'gz'}, dimensions={0}, use_global_device_ids=true | all-gather | bytes 87040 | tf_op jit(solution)/shard_map/all_gather | solution.py:48
  293.2 13.2 %all-gather.1 = f32[64,8,5,32]{3,1,2,0:T(8,128)S(1)} all-gather(f32[16,8,5,32]{3,1,2,0:T(8,128)S(1)} %copy.1162), channel_id=3, replica_groups=mesh['gx_0'=8,'gx_1'=2,'gy'=4,'gz'=16] {'gy'}, dimensions={0}, use_global_device_ids=true | all-gather | bytes 409600 | tf_op jit(solution)/shard_map/all_gather | solution.py:48
  306.3 3.9 all-gather.2
  310.7 4.4 reshape.339
  315.1 3.3 copy.1230
  322.0 3.5 slice.792
  340.3 8.8 %copy.1166 = f32[4,16,8,256]{0,3,2,1:T(8,128)} copy(f32[4,16,8,256]{3,2,1,0:T(8,128)S(1)} %copy-done.11) | data formatting | bytes 1048576 | tf_op jit(solution)/shard_map/sub | solution.py:101
  349.0 12.0 %reduce_sum.121 = f32[4,8,4,128]{0,3,2,1:T(8,128)S(1)} reduce(f32[4,8,2,4,2,128,2]{0,6,5,4,3,2,1:T(2,128)} %bitcast.119, f32[]{:T(128)} %constant.228.clone.1), dimensions={2,4,6}, to_apply=%region_22.23 | reduce | flops 114688 | bytes 589828 | tf_op jit(solution)/shard_map/reduce_sum | solution.py:81
  384.8 3.9 collective-permute-start.38
  390.7 4.9 %collective-permute-start.36 = (f32[4,1,4,32]{0,3,2,1:T(8,128)S(1)}, f32[4,1,4,32]{0,3,2,1:T(8,128)S(1)}, u32[]{:S(2)}, u32[]{:S(2)}) collective-permute-start(f32[4,1,4,32]{0,3,2,1:T(8,128)S(1)} %get-tuple-element.149), channel_id=1, source_target_pairs={{64,0},{128,64},{192,128},{256,192},{320,256},{384,320},{448,384},... | collective-permute-start | bytes 6152 | tf_op jit(solution)/shard_map/ppermute | solution.py:28
  401.5 3.9 collective-permute-done.41
  408.9 3.3 collective-permute-start.44
  414.2 4.9 %collective-permute-start.42 = (f32[4,1,8,64]{3,2,1,0:T(8,128)S(1)}, f32[4,1,8,64]{3,2,1,0:T(8,128)S(1)}, u32[]{:S(2)}, u32[]{:S(2)}) collective-permute-start(f32[4,1,8,64]{3,2,1,0:T(8,128)S(1)} %get-tuple-element.167), channel_id=1, source_target_pairs={{64,0},{128,64},{192,128},{256,192},{320,256},{384,320},{448,384},... | collective-permute-start | bytes 24584 | tf_op jit(solution)/shard_map/ppermute | solution.py:28
  421.0 3.9 collective-permute-start.47
  434.2 3.9 collective-permute-start.51
  440.0 4.9 %collective-permute-start.48 = (f32[4,1,16,128]{3,2,1,0:T(8,128)S(1)}, f32[4,1,16,128]{3,2,1,0:T(8,128)S(1)}, u32[]{:S(2)}, u32[]{:S(2)}) collective-permute-start(f32[4,1,16,128]{3,2,1,0:T(8,128)S(1)} %get-tuple-element.131), channel_id=1, source_target_pairs={{64,0},{128,64},{192,128},{256,192},{320,256},{384,320},{448,384},... | collective-permute-start | bytes 98312 | tf_op jit(solution)/shard_map/ppermute | solution.py:28
  446.8 3.9 collective-permute-start.53
  453.1 3.1 collective-permute-done.53
  458.8 3.9 collective-permute-start.57
  464.7 4.9 %collective-permute-start.54 = (f32[4,1,16,128]{3,2,1,0:T(8,128)S(1)}, f32[4,1,16,128]{3,2,1,0:T(8,128)S(1)}, u32[]{:S(2)}, u32[]{:S(2)}) collective-permute-start(f32[4,1,16,128]{3,2,1,0:T(8,128)S(1)} %get-tuple-element.125), channel_id=1, source_target_pairs={{64,0},{128,64},{192,128},{256,192},{320,256},{384,320},{448,384},... | collective-permute-start | bytes 98312 | tf_op jit(solution)/shard_map/ppermute | solution.py:28
  471.6 3.9 collective-permute-start.59
  477.8 3.2 collective-permute-done.59
  (338 shorter events, 161.4 us)
Async XLA Ops:
  2.6 98.7 %collective-permute-start.2 = (f32[4,8,1,128]{3,1,2,0:T(8,128)S(1)}, f32[4,8,1,128]{3,1,2,0:T(8,128)S(1)}, u32[]{:S(2)}, u32[]{:S(2)}) collective-permute-start(f32[4,8,1,128]{3,1,2,0:T(8,128)S(1)} %bitcast.155), channel_id=1, source_target_pairs={{16,0},{32,16},{48,32},{17,1},{33,17},{49,33},{18,2},{34,18},{50,3... | collective-permute-start | bytes 49160 | tf_op jit(solution)/shard_map/ppermute | solution.py:28
  5.0 99.0 %collective-permute-start.3 = (f32[4,8,1,128]{3,1,2,0:T(8,128)S(1)}, f32[4,8,1,128]{3,1,2,0:T(8,128)S(1)}, u32[]{:S(2)}, u32[]{:S(2)}) collective-permute-start(f32[4,8,1,128]{3,1,2,0:T(8,128)S(1)} %bitcast.154), channel_id=1, source_target_pairs={{0,16},{16,32},{32,48},{1,17},{17,33},{33,49},{2,18},{18,34},{34,5... | collective-permute-start | bytes 49160 | tf_op jit(solution)/shard_map/ppermute | solution.py:27
  8.5 102.3 %collective-permute-start.1 = (f32[4,1,16,128]{3,2,1,0:T(8,128)S(1)}, f32[4,1,16,128]{3,2,1,0:T(8,128)S(1)}, u32[]{:S(2)}, u32[]{:S(2)}) collective-permute-start(f32[4,1,16,128]{3,2,1,0:T(8,128)S(1)} %get-tuple-element.142), channel_id=1, source_target_pairs={{0,64},{64,128},{128,192},{192,256},{256,320},{320,384},{384,448},... | collective-permute-start | bytes 98312 | tf_op jit(solution)/shard_map/ppermute | solution.py:27
  10.4 100.4 %collective-permute-start = (f32[4,1,16,128]{3,2,1,0:T(8,128)S(1)}, f32[4,1,16,128]{3,2,1,0:T(8,128)S(1)}, u32[]{:S(2)}, u32[]{:S(2)}) collective-permute-start(f32[4,1,16,128]{3,2,1,0:T(8,128)S(1)} %get-tuple-element.143), channel_id=1, source_target_pairs={{64,0},{128,64},{192,128},{256,192},{320,256},{384,320},{448,384},... | collective-permute-start | bytes 98312 | tf_op jit(solution)/shard_map/ppermute | solution.py:28
  15.4 88.7 %collective-permute-start.4 = (f32[4,8,16,1]{3,2,1,0:T(8,128)S(1)}, f32[4,8,16,1]{3,2,1,0:T(8,128)S(1)}, u32[]{:S(2)}, u32[]{:S(2)}) collective-permute-start(f32[4,8,16,1]{3,2,1,0:T(8,128)S(1)} %get-tuple-element.140), channel_id=1, source_target_pairs={{1,0},{2,1},{3,2},{4,3},{5,4},{6,5},{7,6},{8,7},{9,8},{10,9},{11,1... | collective-permute-start | bytes 6152 | tf_op jit(solution)/shard_map/ppermute | solution.py:28
  101.3 9.5 %collective-permute-start.5 = (f32[4,8,16,1]{3,2,1,0:T(8,128)S(1)}, f32[4,8,16,1]{3,2,1,0:T(8,128)S(1)}, u32[]{:S(2)}, u32[]{:S(2)}) collective-permute-start(f32[4,8,16,1]{3,2,1,0:T(8,128)S(1)} %get-tuple-element.141), channel_id=1, source_target_pairs={{0,1},{1,2},{2,3},{3,4},{4,5},{5,6},{6,7},{7,8},{8,9},{9,10},{10,1... | collective-permute-start | bytes 6152 | tf_op jit(solution)/shard_map/ppermute | solution.py:27
  111.3 14.6 %collective-permute-start.8 = (f32[4,8,1,128]{3,1,2,0:T(8,128)S(1)}, f32[4,8,1,128]{3,1,2,0:T(8,128)S(1)}, u32[]{:S(2)}, u32[]{:S(2)}) collective-permute-start(f32[4,8,1,128]{3,1,2,0:T(8,128)S(1)} %bitcast.159), channel_id=1, source_target_pairs={{16,0},{32,16},{48,32},{17,1},{33,17},{49,33},{18,2},{34,18},{50,3... | collective-permute-start | bytes 49160 | tf_op jit(solution)/shard_map/ppermute | solution.py:28
  114.4 16.4 %collective-permute-start.9 = (f32[4,8,1,128]{3,1,2,0:T(8,128)S(1)}, f32[4,8,1,128]{3,1,2,0:T(8,128)S(1)}, u32[]{:S(2)}, u32[]{:S(2)}) collective-permute-start(f32[4,8,1,128]{3,1,2,0:T(8,128)S(1)} %bitcast.156), channel_id=1, source_target_pairs={{0,16},{16,32},{32,48},{1,17},{17,33},{33,49},{2,18},{18,34},{34,5... | collective-permute-start | bytes 49160 | tf_op jit(solution)/shard_map/ppermute | solution.py:27
  117.2 19.2 %collective-permute-start.7 = (f32[4,1,16,128]{3,2,1,0:T(8,128)S(1)}, f32[4,1,16,128]{3,2,1,0:T(8,128)S(1)}, u32[]{:S(2)}, u32[]{:S(2)}) collective-permute-start(f32[4,1,16,128]{3,2,1,0:T(8,128)S(1)} %get-tuple-element.136), channel_id=1, source_target_pairs={{0,64},{64,128},{128,192},{192,256},{256,320},{320,384},{384,448},... | collective-permute-start | bytes 98312 | tf_op jit(solution)/shard_map/ppermute | solution.py:27
  119.1 17.3 %collective-permute-start.6 = (f32[4,1,16,128]{3,2,1,0:T(8,128)S(1)}, f32[4,1,16,128]{3,2,1,0:T(8,128)S(1)}, u32[]{:S(2)}, u32[]{:S(2)}) collective-permute-start(f32[4,1,16,128]{3,2,1,0:T(8,128)S(1)} %get-tuple-element.137), channel_id=1, source_target_pairs={{64,0},{128,64},{192,128},{256,192},{320,256},{384,320},{448,384},... | collective-permute-start | bytes 98312 | tf_op jit(solution)/shard_map/ppermute | solution.py:28
  124.0 9.3 %collective-permute-start.10 = (f32[4,8,16,1]{3,2,1,0:T(8,128)S(1)}, f32[4,8,16,1]{3,2,1,0:T(8,128)S(1)}, u32[]{:S(2)}, u32[]{:S(2)}) collective-permute-start(f32[4,8,16,1]{3,2,1,0:T(8,128)S(1)} %get-tuple-element.134), channel_id=1, source_target_pairs={{1,0},{2,1},{3,2},{4,3},{5,4},{6,5},{7,6},{8,7},{9,8},{10,9},{11,1... | collective-permute-start | bytes 6152 | tf_op jit(solution)/shard_map/ppermute | solution.py:28
  125.9 10.5 %collective-permute-start.11 = (f32[4,8,16,1]{3,2,1,0:T(8,128)S(1)}, f32[4,8,16,1]{3,2,1,0:T(8,128)S(1)}, u32[]{:S(2)}, u32[]{:S(2)}) collective-permute-start(f32[4,8,16,1]{3,2,1,0:T(8,128)S(1)} %get-tuple-element.135), channel_id=1, source_target_pairs={{0,1},{1,2},{2,3},{3,4},{4,5},{5,6},{6,7},{7,8},{8,9},{9,10},{10,1... | collective-permute-start | bytes 6152 | tf_op jit(solution)/shard_map/ppermute | solution.py:27
  150.7 15.2 %collective-permute-start.15 = (f32[4,4,1,64]{3,2,1,0:T(1,128)S(1)}, f32[4,4,1,64]{3,2,1,0:T(1,128)S(1)}, u32[]{:S(2)}, u32[]{:S(2)}) collective-permute-start(f32[4,4,1,64]{3,2,1,0:T(1,128)S(1)} %get-tuple-element.180), channel_id=1, source_target_pairs={{0,16},{16,32},{32,48},{1,17},{17,33},{33,49},{2,18},{18,34},{34,5... | collective-permute-start | bytes 12296 | tf_op jit(solution)/shard_map/ppermute | solution.py:27
  152.6 16.7 %collective-permute-start.14 = (f32[4,4,1,64]{3,2,1,0:T(1,128)S(1)}, f32[4,4,1,64]{3,2,1,0:T(1,128)S(1)}, u32[]{:S(2)}, u32[]{:S(2)}) collective-permute-start(f32[4,4,1,64]{3,2,1,0:T(1,128)S(1)} %get-tuple-element.181), channel_id=1, source_target_pairs={{16,0},{32,16},{48,32},{17,1},{33,17},{49,33},{18,2},{34,18},{50,3... | collective-permute-start | bytes 12296 | tf_op jit(solution)/shard_map/ppermute | solution.py:28
  156.5 16.7 %collective-permute-start.13 = (f32[4,1,8,64]{3,2,1,0:T(8,128)S(1)}, f32[4,1,8,64]{3,2,1,0:T(8,128)S(1)}, u32[]{:S(2)}, u32[]{:S(2)}) collective-permute-start(f32[4,1,8,64]{3,2,1,0:T(8,128)S(1)} %get-tuple-element.178), channel_id=1, source_target_pairs={{0,64},{64,128},{128,192},{192,256},{256,320},{320,384},{384,448},... | collective-permute-start | bytes 24584 | tf_op jit(solution)/shard_map/ppermute | solution.py:27
  158.4 14.8 %collective-permute-start.12 = (f32[4,1,8,64]{3,2,1,0:T(8,128)S(1)}, f32[4,1,8,64]{3,2,1,0:T(8,128)S(1)}, u32[]{:S(2)}, u32[]{:S(2)}) collective-permute-start(f32[4,1,8,64]{3,2,1,0:T(8,128)S(1)} %get-tuple-element.179), channel_id=1, source_target_pairs={{64,0},{128,64},{192,128},{256,192},{320,256},{384,320},{448,384},... | collective-permute-start | bytes 24584 | tf_op jit(solution)/shard_map/ppermute | solution.py:28
  173.4 14.7 %collective-permute-start.21 = (f32[4,4,1,64]{3,2,1,0:T(1,128)S(1)}, f32[4,4,1,64]{3,2,1,0:T(1,128)S(1)}, u32[]{:S(2)}, u32[]{:S(2)}) collective-permute-start(f32[4,4,1,64]{3,2,1,0:T(1,128)S(1)} %get-tuple-element.174), channel_id=1, source_target_pairs={{0,16},{16,32},{32,48},{1,17},{17,33},{33,49},{2,18},{18,34},{34,5... | collective-permute-start | bytes 12296 | tf_op jit(solution)/shard_map/ppermute | solution.py:27
  175.4 16.8 %collective-permute-start.20 = (f32[4,4,1,64]{3,2,1,0:T(1,128)S(1)}, f32[4,4,1,64]{3,2,1,0:T(1,128)S(1)}, u32[]{:S(2)}, u32[]{:S(2)}) collective-permute-start(f32[4,4,1,64]{3,2,1,0:T(1,128)S(1)} %get-tuple-element.175), channel_id=1, source_target_pairs={{16,0},{32,16},{48,32},{17,1},{33,17},{49,33},{18,2},{34,18},{50,3... | collective-permute-start | bytes 12296 | tf_op jit(solution)/shard_map/ppermute | solution.py:28
  179.3 16.2 %collective-permute-start.19 = (f32[4,1,8,64]{3,2,1,0:T(8,128)S(1)}, f32[4,1,8,64]{3,2,1,0:T(8,128)S(1)}, u32[]{:S(2)}, u32[]{:S(2)}) collective-permute-start(f32[4,1,8,64]{3,2,1,0:T(8,128)S(1)} %get-tuple-element.172), channel_id=1, source_target_pairs={{0,64},{64,128},{128,192},{192,256},{256,320},{320,384},{384,448},... | collective-permute-start | bytes 24584 | tf_op jit(solution)/shard_map/ppermute | solution.py:27
  181.2 14.3 %collective-permute-start.18 = (f32[4,1,8,64]{3,2,1,0:T(8,128)S(1)}, f32[4,1,8,64]{3,2,1,0:T(8,128)S(1)}, u32[]{:S(2)}, u32[]{:S(2)}) collective-permute-start(f32[4,1,8,64]{3,2,1,0:T(8,128)S(1)} %get-tuple-element.173), channel_id=1, source_target_pairs={{64,0},{128,64},{192,128},{256,192},{320,256},{384,320},{448,384},... | collective-permute-start | bytes 24584 | tf_op jit(solution)/shard_map/ppermute | solution.py:28
  196.9 14.6 %collective-permute-start.27 = (f32[4,2,1,32]{0,3,2,1:T(8,128)S(1)}, f32[4,2,1,32]{0,3,2,1:T(8,128)S(1)}, u32[]{:S(2)}, u32[]{:S(2)}) collective-permute-start(f32[4,2,1,32]{0,3,2,1:T(8,128)S(1)} %get-tuple-element.162), channel_id=1, source_target_pairs={{0,16},{16,32},{32,48},{1,17},{17,33},{33,49},{2,18},{18,34},{34,5... | collective-permute-start | bytes 3080 | tf_op jit(solution)/shard_map/ppermute | solution.py:27
  198.8 16.6 %collective-permute-start.26 = (f32[4,2,1,32]{0,3,2,1:T(8,128)S(1)}, f32[4,2,1,32]{0,3,2,1:T(8,128)S(1)}, u32[]{:S(2)}, u32[]{:S(2)}) collective-permute-start(f32[4,2,1,32]{0,3,2,1:T(8,128)S(1)} %get-tuple-element.163), channel_id=1, source_target_pairs={{16,0},{32,16},{48,32},{17,1},{33,17},{49,33},{18,2},{34,18},{50,3... | collective-permute-start | bytes 3080 | tf_op jit(solution)/shard_map/ppermute | solution.py:28
  202.7 15.5 %collective-permute-start.25 = (f32[4,1,4,32]{0,3,2,1:T(8,128)S(1)}, f32[4,1,4,32]{0,3,2,1:T(8,128)S(1)}, u32[]{:S(2)}, u32[]{:S(2)}) collective-permute-start(f32[4,1,4,32]{0,3,2,1:T(8,128)S(1)} %get-tuple-element.160), channel_id=1, source_target_pairs={{0,64},{64,128},{128,192},{192,256},{256,320},{320,384},{384,448},... | collective-permute-start | bytes 6152 | tf_op jit(solution)/shard_map/ppermute | solution.py:27
  204.7 13.5 %collective-permute-start.24 = (f32[4,1,4,32]{0,3,2,1:T(8,128)S(1)}, f32[4,1,4,32]{0,3,2,1:T(8,128)S(1)}, u32[]{:S(2)}, u32[]{:S(2)}) collective-permute-start(f32[4,1,4,32]{0,3,2,1:T(8,128)S(1)} %get-tuple-element.161), channel_id=1, source_target_pairs={{64,0},{128,64},{192,128},{256,192},{320,256},{384,320},{448,384},... | collective-permute-start | bytes 6152 | tf_op jit(solution)/shard_map/ppermute | solution.py:28
  218.4 14.6 %collective-permute-start.33 = (f32[4,2,1,32]{0,3,2,1:T(8,128)S(1)}, f32[4,2,1,32]{0,3,2,1:T(8,128)S(1)}, u32[]{:S(2)}, u32[]{:S(2)}) collective-permute-start(f32[4,2,1,32]{0,3,2,1:T(8,128)S(1)} %get-tuple-element.156), channel_id=1, source_target_pairs={{0,16},{16,32},{32,48},{1,17},{17,33},{33,49},{2,18},{18,34},{34,5... | collective-permute-start | bytes 3080 | tf_op jit(solution)/shard_map/ppermute | solution.py:27
  220.4 16.6 %collective-permute-start.32 = (f32[4,2,1,32]{0,3,2,1:T(8,128)S(1)}, f32[4,2,1,32]{0,3,2,1:T(8,128)S(1)}, u32[]{:S(2)}, u32[]{:S(2)}) collective-permute-start(f32[4,2,1,32]{0,3,2,1:T(8,128)S(1)} %get-tuple-element.157), channel_id=1, source_target_pairs={{16,0},{32,16},{48,32},{17,1},{33,17},{49,33},{18,2},{34,18},{50,3... | collective-permute-start | bytes 3080 | tf_op jit(solution)/shard_map/ppermute | solution.py:28
  224.3 15.5 %collective-permute-start.31 = (f32[4,1,4,32]{0,3,2,1:T(8,128)S(1)}, f32[4,1,4,32]{0,3,2,1:T(8,128)S(1)}, u32[]{:S(2)}, u32[]{:S(2)}) collective-permute-start(f32[4,1,4,32]{0,3,2,1:T(8,128)S(1)} %get-tuple-element.154), channel_id=1, source_target_pairs={{0,64},{64,128},{128,192},{192,256},{256,320},{320,384},{384,448},... | collective-permute-start | bytes 6152 | tf_op jit(solution)/shard_map/ppermute | solution.py:27
  226.2 13.5 %collective-permute-start.30 = (f32[4,1,4,32]{0,3,2,1:T(8,128)S(1)}, f32[4,1,4,32]{0,3,2,1:T(8,128)S(1)}, u32[]{:S(2)}, u32[]{:S(2)}) collective-permute-start(f32[4,1,4,32]{0,3,2,1:T(8,128)S(1)} %get-tuple-element.155), channel_id=1, source_target_pairs={{64,0},{128,64},{192,128},{256,192},{320,256},{384,320},{448,384},... | collective-permute-start | bytes 6152 | tf_op jit(solution)/shard_map/ppermute | solution.py:28
  382.9 15.8 %collective-permute-start.39 = (f32[4,2,1,32]{0,3,2,1:T(8,128)S(1)}, f32[4,2,1,32]{0,3,2,1:T(8,128)S(1)}, u32[]{:S(2)}, u32[]{:S(2)}) collective-permute-start(f32[4,2,1,32]{0,3,2,1:T(8,128)S(1)} %get-tuple-element.150), channel_id=1, source_target_pairs={{0,16},{16,32},{32,48},{1,17},{17,33},{33,49},{2,18},{18,34},{34,5... | collective-permute-start | bytes 3080 | tf_op jit(solution)/shard_map/ppermute | solution.py:27
  384.8 16.6 %collective-permute-start.38 = (f32[4,2,1,32]{0,3,2,1:T(8,128)S(1)}, f32[4,2,1,32]{0,3,2,1:T(8,128)S(1)}, u32[]{:S(2)}, u32[]{:S(2)}) collective-permute-start(f32[4,2,1,32]{0,3,2,1:T(8,128)S(1)} %get-tuple-element.151), channel_id=1, source_target_pairs={{16,0},{32,16},{48,32},{17,1},{33,17},{49,33},{18,2},{34,18},{50,3... | collective-permute-start | bytes 3080 | tf_op jit(solution)/shard_map/ppermute | solution.py:28
  388.7 16.7 %collective-permute-start.37 = (f32[4,1,4,32]{0,3,2,1:T(8,128)S(1)}, f32[4,1,4,32]{0,3,2,1:T(8,128)S(1)}, u32[]{:S(2)}, u32[]{:S(2)}) collective-permute-start(f32[4,1,4,32]{0,3,2,1:T(8,128)S(1)} %get-tuple-element.148), channel_id=1, source_target_pairs={{0,64},{64,128},{128,192},{192,256},{256,320},{320,384},{384,448},... | collective-permute-start | bytes 6152 | tf_op jit(solution)/shard_map/ppermute | solution.py:27
  390.7 14.7 %collective-permute-start.36 = (f32[4,1,4,32]{0,3,2,1:T(8,128)S(1)}, f32[4,1,4,32]{0,3,2,1:T(8,128)S(1)}, u32[]{:S(2)}, u32[]{:S(2)}) collective-permute-start(f32[4,1,4,32]{0,3,2,1:T(8,128)S(1)} %get-tuple-element.149), channel_id=1, source_target_pairs={{64,0},{128,64},{192,128},{256,192},{320,256},{384,320},{448,384},... | collective-permute-start | bytes 6152 | tf_op jit(solution)/shard_map/ppermute | solution.py:28
  406.4 14.6 %collective-permute-start.45 = (f32[4,4,1,64]{3,2,1,0:T(1,128)S(1)}, f32[4,4,1,64]{3,2,1,0:T(1,128)S(1)}, u32[]{:S(2)}, u32[]{:S(2)}) collective-permute-start(f32[4,4,1,64]{3,2,1,0:T(1,128)S(1)} %get-tuple-element.168), channel_id=1, source_target_pairs={{0,16},{16,32},{32,48},{1,17},{17,33},{33,49},{2,18},{18,34},{34,5... | collective-permute-start | bytes 12296 | tf_op jit(solution)/shard_map/ppermute | solution.py:27
  408.9 17.3 %collective-permute-start.44 = (f32[4,4,1,64]{3,2,1,0:T(1,128)S(1)}, f32[4,4,1,64]{3,2,1,0:T(1,128)S(1)}, u32[]{:S(2)}, u32[]{:S(2)}) collective-permute-start(f32[4,4,1,64]{3,2,1,0:T(1,128)S(1)} %get-tuple-element.169), channel_id=1, source_target_pairs={{16,0},{32,16},{48,32},{17,1},{33,17},{49,33},{18,2},{34,18},{50,3... | collective-permute-start | bytes 12296 | tf_op jit(solution)/shard_map/ppermute | solution.py:28
  412.2 16.1 %collective-permute-start.43 = (f32[4,1,8,64]{3,2,1,0:T(8,128)S(1)}, f32[4,1,8,64]{3,2,1,0:T(8,128)S(1)}, u32[]{:S(2)}, u32[]{:S(2)}) collective-permute-start(f32[4,1,8,64]{3,2,1,0:T(8,128)S(1)} %get-tuple-element.166), channel_id=1, source_target_pairs={{0,64},{64,128},{128,192},{192,256},{256,320},{320,384},{384,448},... | collective-permute-start | bytes 24584 | tf_op jit(solution)/shard_map/ppermute | solution.py:27
  414.2 14.2 %collective-permute-start.42 = (f32[4,1,8,64]{3,2,1,0:T(8,128)S(1)}, f32[4,1,8,64]{3,2,1,0:T(8,128)S(1)}, u32[]{:S(2)}, u32[]{:S(2)}) collective-permute-start(f32[4,1,8,64]{3,2,1,0:T(8,128)S(1)} %get-tuple-element.167), channel_id=1, source_target_pairs={{64,0},{128,64},{192,128},{256,192},{320,256},{384,320},{448,384},... | collective-permute-start | bytes 24584 | tf_op jit(solution)/shard_map/ppermute | solution.py:28
  432.2 14.6 %collective-permute-start.50 = (f32[4,8,1,128]{3,1,2,0:T(8,128)S(1)}, f32[4,8,1,128]{3,1,2,0:T(8,128)S(1)}, u32[]{:S(2)}, u32[]{:S(2)}) collective-permute-start(f32[4,8,1,128]{3,1,2,0:T(8,128)S(1)} %bitcast.160), channel_id=1, source_target_pairs={{16,0},{32,16},{48,32},{17,1},{33,17},{49,33},{18,2},{34,18},{50,3... | collective-permute-start | bytes 49160 | tf_op jit(solution)/shard_map/ppermute | solution.py:28
  434.2 17.3 %collective-permute-start.51 = (f32[4,8,1,128]{3,1,2,0:T(8,128)S(1)}, f32[4,8,1,128]{3,1,2,0:T(8,128)S(1)}, u32[]{:S(2)}, u32[]{:S(2)}) collective-permute-start(f32[4,8,1,128]{3,1,2,0:T(8,128)S(1)} %bitcast.158), channel_id=1, source_target_pairs={{0,16},{16,32},{32,48},{1,17},{17,33},{33,49},{2,18},{18,34},{34,5... | collective-permute-start | bytes 49160 | tf_op jit(solution)/shard_map/ppermute | solution.py:27
  438.1 18.2 %collective-permute-start.49 = (f32[4,1,16,128]{3,2,1,0:T(8,128)S(1)}, f32[4,1,16,128]{3,2,1,0:T(8,128)S(1)}, u32[]{:S(2)}, u32[]{:S(2)}) collective-permute-start(f32[4,1,16,128]{3,2,1,0:T(8,128)S(1)} %get-tuple-element.130), channel_id=1, source_target_pairs={{0,64},{64,128},{128,192},{192,256},{256,320},{320,384},{384,448},... | collective-permute-start | bytes 98312 | tf_op jit(solution)/shard_map/ppermute | solution.py:27
  440.0 16.3 %collective-permute-start.48 = (f32[4,1,16,128]{3,2,1,0:T(8,128)S(1)}, f32[4,1,16,128]{3,2,1,0:T(8,128)S(1)}, u32[]{:S(2)}, u32[]{:S(2)}) collective-permute-start(f32[4,1,16,128]{3,2,1,0:T(8,128)S(1)} %get-tuple-element.131), channel_id=1, source_target_pairs={{64,0},{128,64},{192,128},{256,192},{320,256},{384,320},{448,384},... | collective-permute-start | bytes 98312 | tf_op jit(solution)/shard_map/ppermute | solution.py:28
  444.9 8.3 %collective-permute-start.52 = (f32[4,8,16,1]{3,2,1,0:T(8,128)S(1)}, f32[4,8,16,1]{3,2,1,0:T(8,128)S(1)}, u32[]{:S(2)}, u32[]{:S(2)}) collective-permute-start(f32[4,8,16,1]{3,2,1,0:T(8,128)S(1)} %get-tuple-element.128), channel_id=1, source_target_pairs={{1,0},{2,1},{3,2},{4,3},{5,4},{6,5},{7,6},{8,7},{9,8},{10,9},{11,1... | collective-permute-start | bytes 6152 | tf_op jit(solution)/shard_map/ppermute | solution.py:28
  446.8 9.5 %collective-permute-start.53 = (f32[4,8,16,1]{3,2,1,0:T(8,128)S(1)}, f32[4,8,16,1]{3,2,1,0:T(8,128)S(1)}, u32[]{:S(2)}, u32[]{:S(2)}) collective-permute-start(f32[4,8,16,1]{3,2,1,0:T(8,128)S(1)} %get-tuple-element.129), channel_id=1, source_target_pairs={{0,1},{1,2},{2,3},{3,4},{4,5},{5,6},{6,7},{7,8},{8,9},{9,10},{10,1... | collective-permute-start | bytes 6152 | tf_op jit(solution)/shard_map/ppermute | solution.py:27
  456.9 14.7 %collective-permute-start.56 = (f32[4,8,1,128]{3,1,2,0:T(8,128)S(1)}, f32[4,8,1,128]{3,1,2,0:T(8,128)S(1)}, u32[]{:S(2)}, u32[]{:S(2)}) collective-permute-start(f32[4,8,1,128]{3,1,2,0:T(8,128)S(1)} %bitcast.161), channel_id=1, source_target_pairs={{16,0},{32,16},{48,32},{17,1},{33,17},{49,33},{18,2},{34,18},{50,3... | collective-permute-start | bytes 49160 | tf_op jit(solution)/shard_map/ppermute | solution.py:28
  458.8 18.7 %collective-permute-start.57 = (f32[4,8,1,128]{3,1,2,0:T(8,128)S(1)}, f32[4,8,1,128]{3,1,2,0:T(8,128)S(1)}, u32[]{:S(2)}, u32[]{:S(2)}) collective-permute-start(f32[4,8,1,128]{3,1,2,0:T(8,128)S(1)} %bitcast.157), channel_id=1, source_target_pairs={{0,16},{16,32},{32,48},{1,17},{17,33},{33,49},{2,18},{18,34},{34,5... | collective-permute-start | bytes 49160 | tf_op jit(solution)/shard_map/ppermute | solution.py:27
  462.8 18.3 %collective-permute-start.55 = (f32[4,1,16,128]{3,2,1,0:T(8,128)S(1)}, f32[4,1,16,128]{3,2,1,0:T(8,128)S(1)}, u32[]{:S(2)}, u32[]{:S(2)}) collective-permute-start(f32[4,1,16,128]{3,2,1,0:T(8,128)S(1)} %get-tuple-element.124), channel_id=1, source_target_pairs={{0,64},{64,128},{128,192},{192,256},{256,320},{320,384},{384,448},... | collective-permute-start | bytes 98312 | tf_op jit(solution)/shard_map/ppermute | solution.py:27
  464.7 16.4 %collective-permute-start.54 = (f32[4,1,16,128]{3,2,1,0:T(8,128)S(1)}, f32[4,1,16,128]{3,2,1,0:T(8,128)S(1)}, u32[]{:S(2)}, u32[]{:S(2)}) collective-permute-start(f32[4,1,16,128]{3,2,1,0:T(8,128)S(1)} %get-tuple-element.125), channel_id=1, source_target_pairs={{64,0},{128,64},{192,128},{256,192},{320,256},{384,320},{448,384},... | collective-permute-start | bytes 98312 | tf_op jit(solution)/shard_map/ppermute | solution.py:28
  469.5 8.3 %collective-permute-start.58 = (f32[4,8,16,1]{3,2,1,0:T(8,128)S(1)}, f32[4,8,16,1]{3,2,1,0:T(8,128)S(1)}, u32[]{:S(2)}, u32[]{:S(2)}) collective-permute-start(f32[4,8,16,1]{3,2,1,0:T(8,128)S(1)} %get-tuple-element.122), channel_id=1, source_target_pairs={{1,0},{2,1},{3,2},{4,3},{5,4},{6,5},{7,6},{8,7},{9,8},{10,9},{11,1... | collective-permute-start | bytes 6152 | tf_op jit(solution)/shard_map/ppermute | solution.py:28
  471.6 9.5 %collective-permute-start.59 = (f32[4,8,16,1]{3,2,1,0:T(8,128)S(1)}, f32[4,8,16,1]{3,2,1,0:T(8,128)S(1)}, u32[]{:S(2)}, u32[]{:S(2)}) collective-permute-start(f32[4,8,16,1]{3,2,1,0:T(8,128)S(1)} %get-tuple-element.123), channel_id=1, source_target_pairs={{0,1},{1,2},{2,3},{3,4},{4,5},{5,6},{6,7},{7,8},{8,9},{9,10},{10,1... | collective-permute-start | bytes 6152 | tf_op jit(solution)/shard_map/ppermute | solution.py:27
  (51 other events, 1475.7 us)
where the time goes:
time: 491 us; the launch traced here: 483 us
  starting transfers between devices  183 us (37%)
  blocking collectives  132 us (27%)
  local copies, waits for them, and re-layouts  62.4 us (13%)
  other arithmetic  51.9 us (11%)
  waiting for transfers between devices  39.3 us (8%)
  matrix products  11 us (2%)
    ppermute x30, starting transfers between devices, extended_2(): lax.ppermute(leading, axis, [(b, a) for a, b in up])  102 us
    ppermute x30, starting transfers between devices, extended_2(): lax.ppermute(last, axis, up)  81 us
    all_gather x4, blocking collectives, gather_in_order(): pieces = lax.all_gather(pieces, axes[k])  70.1 us
    psum x4, blocking collectives, over_axes(): return functools.reduce(lax.psum, axes, shard)  62.1 us
    ppermute x30, waiting for transfers between devices, extended_2(): lax.ppermute(last, axis, up)  34.6 us
    reduce_sum x13, other arithmetic, restrict(): field.reshape(depth, size_a // 2, 2, size_b // 2, 2, size_c // 2, 2)  30.7 us
    sub x2, local copies, waits for them, and re-layouts, whole_cycle(): residue = source - stencil(zero_margin(iterate), coeffs, factor)  10.2 us
  transfers between devices with their start and end apart: 60, of which 15 were waited for; matrix products, arithmetic and copies ran while one was open for 6% of the time, Pallas kernels for 0%

commit v1 on v0

v1 whole, which is shorter than its diff:
```python
import functools

import jax
import jax.numpy as jnp
from jax import lax
from jax.experimental import pallas as pl
from jax.experimental.pallas import tpu as pltpu
from jax.sharding import PartitionSpec as P

OMEGA = 0.8
HIGH = lax.Precision.HIGHEST
MESH = pl.DeviceIdType.MESH
KS = OMEGA / 6.0
F32 = jnp.float32
ANY = pl.ANY

G0, V0, G1, V1, G2, V2, C2, C1, C0 = range(9)


def iota(shape, dim):
    return lax.broadcasted_iota(jnp.int32, shape, dim)


def roll(x, shift, axis):
    n = x.shape[axis]
    shift = shift % n
    return x if shift == 0 else pltpu.roll(x, shift, axis)


def partner_sum(x, axis, s):
    low = (iota(x.shape, axis) & s) == 0
    return x + jnp.where(low, roll(x, x.shape[axis] - s, axis), roll(x, s, axis))


def coarsen(x, s):
    pairs = x.reshape(*x.shape[:-3], x.shape[-3] // 2, 2, *x.shape[-2:])
    x = pairs[..., 0, :, :] + pairs[..., 1, :, :]
    x = partner_sum(x, x.ndim - 2, s)
    return partner_sum(x, x.ndim - 1, s) * 0.125


def kernel(nx, ny, nz, old_hbm, prev_hbm, inc_hbm, coef_hbm,
           ortho_hbm, proj_ref, tri_ref, prec_hbm, oper_hbm,
           old, prev, inc, coef, ortho, oper,
           g0, v0, s0, b1, g1, v1, s1, b2, g2, v2, s2, e2, e1, e0, c1, c2,
           xr, ys, yr, zs, zr, row_s, row_r, plane, zb, gz_s, gz_r,
           cc3, inv3, cc4, inv4, inv5, ebuf,
           in_sem, out_sem, x_send, x_recv, y_send, y_recv, z_send, z_recv,
           ax_send, ax_recv, ay_send, ay_recv, az_send, az_recv, ag_send, ag_recv):
    gx, gy, gz = lax.axis_index("gx"), lax.axis_index("gy"), lax.axis_index("gz")
    X, Y, Z = 8, 16, 128

    def at(dx=0, dy=0, dz=0):
        return (lax.rem(gx + dx + nx, nx), lax.rem(gy + dy + ny, ny), lax.rem(gz + dz + nz, nz))

    loads = [
        pltpu.make_async_copy(src, dst, in_sem.at[i])
        for i, (src, dst) in enumerate(((coef_hbm, coef), (inc_hbm, inc), (old_hbm, old), (prev_hbm, prev)))
    ]
    for load in loads:
        load.start()

    for cond, buf, side in ((gx == 0, xr, 0), (gx == nx - 1, xr, 1), (gy == 0, yr, 0), (gy == ny - 1, yr, 1),
                            (gz == 0, zr, 0), (gz == nz - 1, zr, 1)):
        @pl.when(cond)
        def _():
            buf[side] = jnp.zeros(buf.shape[1:], F32)
    for d in (-2, -1, 1, 2):
        @pl.when((gz + d < 0) | (gz + d >= nz))
        def _():
            zb[:, 2 + d] = jnp.zeros((2,) + zb.shape[2:], F32)

    barrier = pltpu.get_barrier_semaphore()
    for d in range(1, nx):
        pl.semaphore_signal(barrier, inc=1, device_id=at(dx=d), device_id_type=MESH)
    for d in range(1, ny):
        pl.semaphore_signal(barrier, inc=1, device_id=at(dy=d), device_id_type=MESH)
    for d in range(1, nz):
        pl.semaphore_signal(barrier, inc=1, device_id=at(dz=d), device_id_type=MESH)

    ebuf[:, 0] = jnp.zeros(ebuf.shape[:1] + ebuf.shape[2:], F32)
    ebuf[:, ny + 1] = jnp.zeros(ebuf.shape[:1] + ebuf.shape[2:], F32)
    ebuf[:, 1:ny + 1, 0:8] = jnp.zeros((8, ny, 8, Z), F32)
    ebuf[:, 1:ny + 1, 8 + nx:] = jnp.zeros((8, ny, 8, Z), F32)

    lane8, row8 = iota((8, Z), 1), iota((8, Z), 0)
    take_ends = (((row8 == 0) & (lane8 == Z - 1)) | ((row8 == 1) & (lane8 == 0))).astype(F32)

    def faces(e, f, n):
        k = n // 2
        out = []
        for side, d in ((0, 1), (1, -1)):
            def copy(src, dst, ssem, rsem, to):
                return pltpu.make_async_remote_copy(src_ref=src, dst_ref=dst, send_sem=ssem, recv_sem=rsem,
                                                    device_id=to, device_id_type=MESH)
            out.append((copy(zs.at[side, e, pl.ds(0, k)], zr.at[side, e, pl.ds(0, k)], z_send.at[side, e],
                             z_recv.at[side, e], at(dz=d)),
                        (gz + d >= 0) & (gz + d < nz), (gz - d >= 0) & (gz - d < nz)))
            out.append((copy(ys.at[side, e, :, pl.ds(0, n)], yr.at[side, e, :, pl.ds(0, n)], y_send.at[side, e],
                             y_recv.at[side, e], at(dy=d)),
                        (gy + d >= 0) & (gy + d < ny), (gy - d >= 0) & (gy - d < ny)))
            out.append((copy(f.at[:, (n - 1) if side == 0 else 0], xr.at[side, e], x_send.at[side, e],
                             x_recv.at[side, e], at(dx=d)),
                        (gx + d >= 0) & (gx + d < nx), (gx - d >= 0) & (gx - d < nx)))
        return out

    sent = []

    def send(e, f, n):
        k, per = n // 2, 8 // n
        for c in range(k):
            rows = f[c * per:(c + 1) * per].reshape(128, Z)
            ends = lax.dot_general(take_ends, rows, (((1,), (1,)), ((), ())), precision=HIGH,
                                   preferred_element_type=F32)
            zs[0, e, c] = ends[0:1]
            zs[1, e, c] = ends[1:2]
        ys[0, e, :, 0:n] = f[:, :, Y - 1:Y, :]
        ys[1, e, :, 0:n] = f[:, :, 0:1, :]
        for copy, sends, _ in faces(e, f, n):
            sent.append((copy, sends))

            @pl.when(sends)
            def _():
                copy.start()

    def receive(e, f, n):
        for copy, _, receives in faces(e, f, n):
            @pl.when(receives)
            def _():
                copy.wait_recv()

    def along_yz(e, f, n, s, c):
        per = 8 // n
        shape = (per, n, Y, Z)
        x = f[c * per:(c + 1) * per]
        row, lane = iota(shape, 2), iota(shape, 3)
        lo, hi = (yr[side, e, c * per:(c + 1) * per, 0:n] for side in (0, 1))
        total = jnp.where(row >= s, roll(x, s, 2), lo) + jnp.where(row < Y - s, roll(x, Y - s, 2), hi)
        total = total + jnp.where(lane >= s, roll(x, s, 3), 0.0) + jnp.where(lane < Z - s, roll(x, Z - s, 3), 0.0)
        ends = jnp.where(row8 == 0, zr[0, e, c], jnp.where(row8 == 1, zr[1, e, c], 0.0))
        put = (((row8 == 0) & (lane8 < s)) | ((row8 == 1) & (lane8 >= Z - s))).astype(F32)
        halo = lax.dot_general(ends, put, (((0,), (0,)), ((), ())), precision=HIGH, preferred_element_type=F32)
        return x, total + halo.reshape(shape)

    def x_ends(e, n, c):
        per = 8 // n
        return (xr[side, e, c * per:(c + 1) * per][:, None] for side in (0, 1))

    def neighbours(e, f, n, s, c):
        x, total = along_yz(e, f, n, s, c)
        lo, hi = x_ends(e, n, c)
        if n > 1:
            lo = jnp.concatenate([lo, x[:, :-1]], axis=1)
            hi = jnp.concatenate([x[:, 1:], hi], axis=1)
        return x, total + lo + hi

    def second_sweep(e, g, v, n, s):
        receive(e, g, n)
        per = 8 // n
        for c in range(n // 2):
            x, near = neighbours(e, g, n, s, c)
            v[c * per:(c + 1) * per] = 1.2 * x + KS * near

    def residual(e, b, c_hat, g, v, third, n, s, put):
        receive(e, v, n)
        per = 8 // n
        for c in range(n // 2):
            part = slice(c * per, (c + 1) * per)
            x, near = neighbours(e, v, n, s, c)
            third[part] = 0.2 * x + g[part] + KS * near
            put(part, coarsen(b[part] - c_hat * (6.0 * x - near), s))

    def corrected(e, coarse, third, out, n, s):
        receive(e, coarse, n)
        per = 8 // n
        for c in range(n // 2):
            part = slice(c * per, (c + 1) * per)
            x, near = along_yz(e, coarse, n, s, c)
            near = near + x
            lo, hi = x_ends(e, n, c)
            if n > 1:
                lo = jnp.concatenate([lo, x[:, :-1]], axis=1)
                hi = jnp.concatenate([x[:, 1:], hi], axis=1)
            both = jnp.stack([0.2 * x + KS * (near + lo), 0.2 * x + KS * (near + hi)], axis=2)
            out[part] = third[part] + both.reshape(per, 2 * n, Y, Z)

    def line_copies(k):
        return [pltpu.make_async_remote_copy(
            src_ref=row_s.at[k], dst_ref=row_r.at[k, gx], send_sem=ax_send.at[k, d - 1], recv_sem=ax_recv.at[k, d - 1],
            device_id=at(dx=d), device_id_type=MESH) for d in range(1, nx)]

    def plane_copies(k):
        return [pltpu.make_async_remote_copy(
            src_ref=plane.at[k, gy], dst_ref=plane.at[k, gy], send_sem=ay_send.at[k, d - 1],
            recv_sem=ay_recv.at[k, d - 1], device_id=at(dy=d), device_id_type=MESH) for d in range(1, ny)]

    def deep_copies(k):
        return [(pltpu.make_async_remote_copy(
            src_ref=plane.at[k], dst_ref=zb.at[k, 2 - d], send_sem=az_send.at[k, i], recv_sem=az_recv.at[k, i],
            device_id=at(dz=d), device_id_type=MESH), (gz + d >= 0) & (gz + d < nz), (gz - d >= 0) & (gz - d < nz))
            for i, d in enumerate((-2, -1, 1, 2))]

    def start_line(k, row):
        row_s[k] = row
        row_r[k, gx] = row
        for copy in line_copies(k):
            copy.start()

    def start_plane(k):
        for copy in line_copies(k):
            copy.wait()
        plane[k, gy] = row_r[k].reshape(nx, Z)
        for copy in plane_copies(k):
            copy.start()

    def start_deep(k):
        for copy in plane_copies(k):
            copy.wait()
        for copy, sends, _ in deep_copies(k):
            @pl.when(sends)
            def _():
                copy.start()
        zb[k, 2] = plane[k]

    def finish_deep(k):
        for copy, _, receives in deep_copies(k):
            @pl.when(receives)
            def _():
                copy.wait_recv()

    def to_row(blocks):
        q = blocks.shape[0]
        rows = jnp.zeros((8, Z), F32)
        for i in range(q):
            rows = jnp.where(row8 == i, blocks[i], rows)
        pick = (iota((Z, Z), 0) == 8 * (iota((Z, Z), 1) % 16)).astype(F32)
        rows = lax.dot_general(rows, pick, (((1,), (0,)), ((), ())), precision=HIGH, preferred_element_type=F32)
        return jnp.sum(jnp.where(lane8 // 16 == row8, rows, 0.0), axis=0, keepdims=True)

    def spread(k, q):
        shape = (ny, nx, Z)
        group = iota(shape, 2) // 16
        out = jnp.zeros(shape, F32)
        for i in range(5):
            out = jnp.where(group == i, roll(zb[k, i], 16 * (i - q), 2), out)
        return out

    loads[0].wait()
    loads[1].wait()
    c_fine = coef[...]
    scale = KS / c_fine
    for v in range(4):
        g0[v] = inc[v] * scale
    c1[...] = coarsen(c_fine, 1)
    c2[...] = coarsen(c1[...], 2)
    c3 = coarsen(c2[...], 4)

    total_devices = (nx - 1) + (ny - 1) + (nz - 1)
    pl.semaphore_wait(barrier, total_devices)
    send(G0, g0, 8)

    loads[2].wait()
    loads[3].wait()
    pairs = [("p", m, j) for m in range(4) for j in range(4)]
    pairs += [("s", i, j) for i in range(4) for j in range(i, 4)]
    pairs += [("c", i, j) for i in range(4) for j in range(i, 4)]
    sums = [None] * len(pairs)
    for x in range(X):
        vo = [old[m, x] for m in range(4)]
        vp = [prev[m, x] for m in range(4)]
        for p, (kind, i, j) in enumerate(pairs):
            a = (vp if kind == "s" else vo)[i]
            b = (vo if kind == "c" else vp)[j]
            ab = a * b
            ab = ab[0:8] + ab[8:16]
            sums[p] = ab if sums[p] is None else sums[p] + ab
    rows = [jnp.sum(a, axis=0, keepdims=True) for a in sums] + [jnp.zeros((4, Z), F32)]
    rows = jnp.sum(jnp.concatenate(rows, axis=0), axis=1, keepdims=True)
    at_lane = iota((40, Z), 1) == iota((40, Z), 0) + 64
    gram_row = jnp.sum(jnp.where(at_lane, rows, 0.0), axis=0, keepdims=True)
    start_line(0, to_row(c3.reshape(2, 8, Z)) + gram_row)

    second_sweep(G0, g0, v0, 8, 1)
    send(V0, v0, 8)
    start_plane(0)

    def put_b1(part, r):
        b1[part] = r
        g1[part] = r * scale1
    scale1 = (4.0 * KS) / c1[...]
    residual(V0, inc, c_fine, g0, v0, s0, 8, 1, put_b1)
    send(G1, g1, 4)
    start_deep(0)
    gram_line = jnp.sum(plane[0].reshape(ny * nx, Z), axis=0, keepdims=True)
    gz_s[...] = gram_line
    gz_r[gz] = gram_line
    gram_copies = [pltpu.make_async_remote_copy(
        src_ref=gz_s, dst_ref=gz_r.at[gz], send_sem=ag_send.at[d - 1], recv_sem=ag_recv.at[d - 1],
        device_id=at(dz=d), device_id_type=MESH) for d in range(1, nz)]
    for copy in gram_copies:
        copy.start()

    second_sweep(G1, g1, v1, 4, 2)
    send(V1, v1, 4)
    scale2 = (16.0 * KS) / c2[...]

    def put_b2(part, r):
        b2[part] = r
        g2[part] = r * scale2
    residual(V1, b1, 0.25 * c1[...], g1, v1, s1, 4, 2, put_b2)
    send(G2, g2, 2)
    second_sweep(G2, g2, v2, 2, 4)
    send(V2, v2, 2)
    held = []
    residual(V2, b2, 0.0625 * c2[...], g2, v2, s2, 2, 4, lambda part, r: held.append(r))
    start_line(1, to_row(held[0].reshape(8, 8, Z)))

    shape = (ny, nx, Z)
    lanes = iota(shape, 2)
    place = (gz - 2) * 16 + lanes
    inside = (place >= 0) & (place < nz * 16) & (lanes < 80)
    km = jnp.where(inside, KS, 0.0)
    finish_deep(0)
    c3g = [jnp.where(inside, spread(0, q), 1.0) for q in range(2)]
    for q in range(2):
        cc3[q] = (1.0 / 64) * c3g[q]
        inv3[q] = jnp.where(inside, (64.0 * KS) / c3g[q], 0.0)

    def coarsen_gathered(x, s):
        x = partner_sum(x, 1, s)
        return partner_sum(x, 2, s) * 0.125
    c4g = coarsen_gathered(c3g[0] + c3g[1], 1)
    cc4[...] = (1.0 / 256) * c4g
    inv4[...] = jnp.where(inside, (256.0 * KS) / c4g, 0.0)
    halved = c4g.reshape(ny // 2, 2, nx, Z)
    c5g = coarsen_gathered(halved[:, 0] + halved[:, 1], 2)
    inv5[...] = jnp.where(inside[:ny // 2], (1024.0 * KS) / c5g, 0.0)

    start_plane(1)

    for copy in gram_copies:
        copy.wait()
    line = jnp.sum(gz_r[...].reshape(nz, Z), axis=0, keepdims=True)
    column = jnp.sum(jnp.where(at_lane, line, 0.0), axis=1, keepdims=True)
    column = column * (1.0 / float(nx * ny * nz * X * Y * Z))
    value = {key: column[p:p + 1] for p, key in enumerate(pairs)}
    for kind in "sc":
        for i in range(4):
            for j in range(i):
                value[kind, i, j] = value[kind, j, i]
    proj = [[value["p", m, j] for j in range(4)] for m in range(4)]
    mixed = [[sum(value["c", m, n] * proj[n][j] for n in range(4)) for j in range(4)] for m in range(4)]
    low = [[None] * 4 for _ in range(4)]
    inverse = [[None] * 4 for _ in range(4)]
    for j in range(4):
        for i in range(j, 4):
            g = value["s", i, j] + sum(proj[m][i] * (mixed[m][j] - 2.0 * proj[m][j]) for m in range(4))
            for k in range(j):
                g = g - low[i][k] * low[j][k]
            low[i][j] = jnp.sqrt(g) if i == j else g / low[j][j]
    for j in range(4):
        inverse[j][j] = 1.0 / low[j][j]
        for i in range(j + 1, 4):
            inverse[i][j] = -sum(low[i][k] * inverse[k][j] for k in range(j, i)) * (1.0 / low[i][i])
    r4, l4 = iota((4, 4), 0), iota((4, 4), 1)
    out_p, out_t = jnp.zeros((4, 4), F32), jnp.zeros((4, 4), F32)
    for i in range(4):
        for j in range(4):
            here = (r4 == i) & (l4 == j)
            out_p = jnp.where(here, proj[i][j], out_p)
            if j >= i:
                out_t = jnp.where(here, low[j][i], out_t)
    proj_ref[...] = out_p
    tri_ref[...] = out_t
    wide = lambda a: jnp.broadcast_to(a, (8, Z))
    proj_w = [[wide(a) for a in line_] for line_ in proj]
    inv_w = [[wide(inverse[j][i]) if i <= j else None for i in range(4)] for j in range(4)]
    for x in range(X):
        for h in range(2):
            part = slice(8 * h, 8 * h + 8)
            vo = [old[m, x, part] for m in range(4)]
            rem = [prev[j, x, part] - sum(proj_w[m][j] * vo[m] for m in range(4)) for j in range(4)]
            for j in range(4):
                ortho[j, x, part] = sum(inv_w[j][i] * rem[i] for i in range(j + 1))
    outs = [pltpu.make_async_copy(ortho, ortho_hbm, out_sem.at[0])]
    outs[0].start()

    start_deep(1)
    finish_deep(1)

    rows_i = iota(shape, 1)
    zero = jnp.zeros((1, nx, Z), F32)

    def along_xz(v, s):
        r = rows_i[:v.shape[0]]
        out = jnp.where(r >= s, roll(v, s, 1), 0.0) + jnp.where(r < nx - s, roll(v, nx - s, 1), 0.0)
        return out + roll(v, s, 2) + roll(v, Z - s, 2)

    def up(v):
        return zero if v.shape[0] == 1 else jnp.concatenate([v[1:], zero], axis=0)

    def down(v):
        return zero if v.shape[0] == 1 else jnp.concatenate([zero, v[:-1]], axis=0)

    def near3(v):
        return [along_xz(v[0], 1) + v[1] + down(v[1]), along_xz(v[1], 1) + v[0] + up(v[0])]

    def near_coarse(v, s):
        return along_xz(v, s) + up(v) + down(v)

    km5 = km[:ny // 2]
    for vec in range(4):
        b = [spread(1, 2 * vec + q) for q in range(2)]
        g = [b[q] * inv3[q] for q in range(2)]
        near = near3(g)
        v = [1.2 * g[q] + km * near[q] for q in range(2)]
        near = near3(v)
        third = [0.2 * v[q] + g[q] + km * near[q] for q in range(2)]
        r = [b[q] - cc3[q] * (6.0 * v[q] - near[q]) for q in range(2)]
        b4 = coarsen_gathered(jnp.where(inside, r[0] + r[1], 0.0), 1)
        g4 = b4 * inv4[...]
        v4 = 1.2 * g4 + km * near_coarse(g4, 2)
        n4 = near_coarse(v4, 2)
        third4 = 0.2 * v4 + g4 + km * n4
        r4_ = b4 - cc4[...] * (6.0 * v4 - n4)
        r4_ = jnp.where(inside, r4_, 0.0).reshape(ny // 2, 2, nx, Z)
        g5 = coarsen_gathered(r4_[:, 0] + r4_[:, 1], 2) * inv5[...]
        v5 = g5
        for _ in range(3):
            v5 = 0.2 * v5 + g5 + km5 * near_coarse(v5, 4)
        p4 = jnp.stack([v5, v5], axis=1).reshape(ny, nx, Z)
        e4 = third4 + 0.2 * p4 + km * near_coarse(p4, 2)
        xz = along_xz(e4, 1) + 1.2 / 6.0 * 0.0
        ebuf[2 * vec, 1:ny + 1, 8:8 + nx] = third[0] + 0.2 * e4 + km * (xz + e4 + down(e4))
        ebuf[2 * vec + 1, 1:ny + 1, 8:8 + nx] = third[1] + 0.2 * e4 + km * (xz + e4 + up(e4))

    def cells(dy, dx):
        return ebuf[:, gy + 1 + dy, pl.ds(8 + gx + dx, 1), :].reshape(8, Z)
    li, lj = iota((Z, Z), 0), iota((Z, Z), 1)
    widen = (li == 32 + lj // 8).astype(F32)
    beside = ((li == 31 + (lj + 4) // 8) | (li == 32 + (lj + 4) // 8)).astype(F32)
    own = cells(0, 0)
    stacked = jnp.concatenate([own, cells(0, -1), cells(0, 1), cells(-1, 0), cells(1, 0)], axis=0)
    wide_rows = lax.dot_general(stacked, widen, (((1,), (0,)), ((), ())), precision=HIGH, preferred_element_type=F32)
    z_rows = lax.dot_general(own, beside, (((1,), (0,)), ((), ())), precision=HIGH, preferred_element_type=F32)
    for vec in range(4):
        q = [2 * vec, 2 * vec + 1]
        a = [wide(wide_rows[i:i + 1]) for i in q]
        x_lo = [wide(wide_rows[8 + i:9 + i]) for i in q]
        x_hi = [wide(wide_rows[16 + i:17 + i]) for i in q]
        y_lo = wide(wide_rows[24 + q[1]:25 + q[1]])
        y_hi = wide(wide_rows[32 + q[0]:33 + q[0]])
        z_sum = [wide(z_rows[i:i + 1]) for i in q]
        mid = a[0] + a[1]
        y_sum = [jnp.where(row8 < 4, y_lo + a[0], mid), jnp.where(row8 < 4, mid, a[1] + y_hi)]
        for h in range(2):
            part = slice(8 * h, 8 * h + 8)
            base = 0.2 * a[h] + KS * (y_sum[h] + z_sum[h] + a[h])
            e2[vec, 0, part] = s2[vec, 0, part] + base + KS * x_lo[h]
            e2[vec, 1, part] = s2[vec, 1, part] + base + KS * x_hi[h]

    send(C2, e2, 2)
    corrected(C2, e2, s1, e1, 2, 2)
    send(C1, e1, 4)
    corrected(C1, e1, s0, e0, 4, 1)
    send(C0, e0, 8)
    outs.append(pltpu.make_async_copy(e0, prec_hbm, out_sem.at[1]))
    outs[1].start()
    receive(C0, e0, 8)
    for c in range(4):
        x, near = neighbours(C0, e0, 8, 1, c)
        oper[c:c + 1] = c_fine * (6.0 * x - near)
    outs.append(pltpu.make_async_copy(oper, oper_hbm, out_sem.at[2]))
    outs[2].start()
    for copy, sends in sent:
        @pl.when(sends)
        def _():
            copy.wait_send()
    for k in range(2):
        for copy, sends, _ in deep_copies(k):
            @pl.when(sends)
            def _():
                copy.wait_send()
    for out in outs:
        out.wait()


def per_device(shape, old_basis, previous, incoming, coefficient):
    nx, ny, nz = shape
    big = pltpu.VMEM((4, 8, 16, 128), F32)
    mid = pltpu.VMEM((4, 4, 16, 128), F32)
    low = pltpu.VMEM((4, 2, 16, 128), F32)
    dma = pltpu.SemaphoreType.DMA
    vm = lambda *s: pltpu.VMEM(s, F32)
    whole = jax.ShapeDtypeStruct((4, 8, 16, 128), F32)
    small = jax.ShapeDtypeStruct((4, 4), F32)
    any_spec = pl.BlockSpec(memory_space=pl.ANY)
    vmem_spec = pl.BlockSpec(memory_space=pltpu.VMEM)
    return pl.pallas_call(
        functools.partial(kernel, nx, ny, nz),
        out_shape=(whole, small, small, whole, whole),
        in_specs=[any_spec] * 4,
        out_specs=(any_spec, vmem_spec, vmem_spec, any_spec, any_spec),
        scratch_shapes=[
            big, big, big, vm(8, 16, 128), big, big,
            big, big, big, mid, mid, mid, mid, low, low, low, low, low, mid, big, vm(4, 16, 128), vm(2, 16, 128),
            vm(2, 9, 4, 16, 128), vm(2, 9, 4, 8, 1, 128), vm(2, 9, 4, 8, 1, 128),
            vm(2, 9, 4, 1, 128), vm(2, 9, 4, 1, 128),
            vm(2, 1, 128), vm(2, nx, 1, 128), vm(2, ny, nx, 128), vm(2, 5, ny, nx, 128), vm(1, 128), vm(nz, 1, 128),
            vm(2, ny, nx, 128), vm(2, ny, nx, 128), vm(ny, nx, 128), vm(ny, nx, 128), vm(ny // 2, nx, 128),
            vm(8, ny + 2, nx + 16, 128),
            dma((4,)), dma((3,)), dma((2, 9)), dma((2, 9)), dma((2, 9)), dma((2, 9)), dma((2, 9)), dma((2, 9)),
            dma((2, nx - 1)), dma((2, nx - 1)), dma((2, ny - 1)), dma((2, ny - 1)), dma((2, 4)), dma((2, 4)),
            dma((nz - 1,)), dma((nz - 1,)),
        ],
        compiler_params=pltpu.CompilerParams(collective_id=0, has_side_effects=True),
    )(old_basis, previous, incoming, coefficient)


def solution(mesh):
    shape = (mesh.shape["gx"], mesh.shape["gy"], mesh.shape["gz"])
    split = P(None, "gx", "gy", "gz")
    return jax.shard_map(
        functools.partial(per_device, shape), mesh=mesh,
        in_specs=(split, split, split, P("gx", "gy", "gz")),
        out_specs=(split, P(), P(), split, split), check_vma=False,
    )
```

time: 491 us -> 81.7 us (0.17)
  the two profiles are of different devices: /device:TPU:290 before, /device:TPU:1 now
where the time goes in v1:
time: 81.7 us; the launch traced here: 81.5 us
  Pallas kernels  76.1 us (93%)
  local copies, waits for them, and re-layouts  4.73 us (6%)
    pallas_call x1, Pallas kernels, per_device(): pl.pallas_call(functools.partial(kernel, nx, ny, nz), out_shape=(whole, s...  76.1 us
    unnamed x13, local copies, waits for them, and re-layouts  4.73 us

profile of v1, /device:TPU:1, one launch (start us, length us, event | category | flops | bytes accessed | tf_op | source)
XLA Modules:
  0.0 81.5 jit_solution(12555171814613901296)
XLA Ops:
  0.6 76.1 %shard_map.83 = (f32[4,8,16,128]{3,2,1,0:T(8,128)}, f32[4,4]{1,0:T(4,128)}, f32[4,4]{1,0:T(4,128)}, f32[4,8,16,128]{3,2,1,0:T(8,128)}, f32[4,8,16,128]{3,2,1,0:T(8,128)}) custom-call(f32[4,8,16,128]{3,2,1,0:T(8,128)} %old_hbm.1, f32[4,8,16,128]{3,2,1,0:T(8,128)} %prev_hbm.1, f32[4,8,16,128]{3,2,1,0:T(8,128)} %inc_hbm.1, f32[8,16,128]{2,1,0:T(8,128)} %coef_hbm.1), custom_call_target="tpu_custom_call" | custom-call | tf_op jit(solution)/shard_map/pallas_call | solution.py:499
  76.7 0.0 copy-start.3
  76.8 0.0 copy-start.1
  76.8 1.7 %copy.14 = f32[4,8,16,128]{3,2,1,0:T(8,128)} copy(f32[4,8,16,128]{3,2,1,0:T(8,128)} %get-tuple-element.10) | data formatting | bytes 524288
  78.5 0.0 copy-done.3
  78.5 0.0 copy-start.2
  78.5 0.6 copy.15
  79.1 0.1 copy-done.2
  79.2 0.6 copy.16
  79.7 0.0 copy-done.1
  79.7 0.0 copy-start
  79.7 0.7 copy.17
  80.5 0.3 copy-done
  80.8 0.7 copy.18
Async XLA Ops:
  76.7 1.7 %copy-start.3 = (f32[4,4]{1,0:T(4,128)S(1)}, f32[4,4]{1,0:T(4,128)}, u32[]{:S(2)}) copy-start(f32[4,4]{1,0:T(4,128)} %get-tuple-element.11) | copy-start | bytes 196
  76.8 3.0 %copy-start.1 = (f32[4,8,16,128]{3,2,1,0:T(8,128)S(1)}, f32[4,8,16,128]{3,2,1,0:T(8,128)}, u32[]{:S(2)}) copy-start(f32[4,8,16,128]{3,2,1,0:T(8,128)} %get-tuple-element.13) | copy-start | bytes 786436
  78.5 0.7 copy-start.2
  79.7 1.0 %copy-start = (f32[4,8,16,128]{3,2,1,0:T(8,128)S(1)}, f32[4,8,16,128]{3,2,1,0:T(8,128)}, u32[]{:S(2)}) copy-start(f32[4,8,16,128]{3,2,1,0:T(8,128)} %get-tuple-element.14) | copy-start | bytes 786436

commit v2 on v1

--- a/solution.py
+++ b/solution.py
@@ -14,7 +14,7 @@
 F32 = jnp.float32
 ANY = pl.ANY
 
-G0, V0, G1, V1, G2, V2, C2, C1, C0 = range(9)
+G0, V0, G1, V1, G2, V2, T2, C1, C0, C2 = range(10)
 
 
 def iota(shape, dim):
@@ -40,13 +40,13 @@
 
 
 def kernel(nx, ny, nz, old_hbm, prev_hbm, inc_hbm, coef_hbm,
-           ortho_hbm, proj_ref, tri_ref, prec_hbm, oper_hbm,
-           old, prev, inc, coef, ortho, oper,
-           g0, v0, s0, b1, g1, v1, s1, b2, g2, v2, s2, e2, e1, e0, c1, c2,
-           xr, ys, yr, zs, zr, row_s, row_r, plane, zb, gz_s, gz_r,
+           ortho, proj_ref, tri_ref, e0, oper,
+           old, prev, inc, coef,
+           g0, v0, s0, b1, g1, v1, s1, b2, g2, v2, s2, e2, e1, c1, c2, beyond,
+           xs, xc, xr, ys, yr, zs, zr, row_s, row_r, line_b, zb, gz_s, gz_r,
            cc3, inv3, cc4, inv4, inv5, ebuf,
-           in_sem, out_sem, x_send, x_recv, y_send, y_recv, z_send, z_recv,
-           ax_send, ax_recv, ay_send, ay_recv, az_send, az_recv, ag_send, ag_recv):
+           in_sem, x_send, x_recv, y_send, y_recv, z_send, z_recv,
+           ax_send, ax_recv, az_send, az_recv, ag_send, ag_recv):
     gx, gy, gz = lax.axis_index("gx"), lax.axis_index("gy"), lax.axis_index("gz")
     X, Y, Z = 8, 16, 128
 
@@ -60,7 +60,7 @@
     for load in loads:
         load.start()
 
-    for cond, buf, side in ((gx == 0, xr, 0), (gx == nx - 1, xr, 1), (gy == 0, yr, 0), (gy == ny - 1, yr, 1),
+    for cond, buf, side in ((gx == 0, xr, 0), (gx == nx - 1, xr, 1), (gx == 0, xc, 0), (gx == nx - 1, xc, 1), (gy == 0, yr, 0), (gy == ny - 1, yr, 1),
                             (gz == 0, zr, 0), (gz == nz - 1, zr, 1)):
         @pl.when(cond)
         def _():
@@ -73,10 +73,17 @@
     barrier = pltpu.get_barrier_semaphore()
     for d in range(1, nx):
         pl.semaphore_signal(barrier, inc=1, device_id=at(dx=d), device_id_type=MESH)
-    for d in range(1, ny):
-        pl.semaphore_signal(barrier, inc=1, device_id=at(dy=d), device_id_type=MESH)
     for d in range(1, nz):
         pl.semaphore_signal(barrier, inc=1, device_id=at(dz=d), device_id_type=MESH)
+    partners = jnp.int32(nx - 1 + nz - 1)
+    for dz in range(-2, 3):
+        reach = (gz + dz >= 0) & (gz + dz < nz)
+        partners = partners + jnp.where(reach, ny - 1, 0)
+
+        @pl.when(reach)
+        def _():
+            for dy in range(1, ny):
+                pl.semaphore_signal(barrier, inc=1, device_id=at(dy=dy, dz=dz), device_id_type=MESH)
 
     ebuf[:, 0] = jnp.zeros(ebuf.shape[:1] + ebuf.shape[2:], F32)
     ebuf[:, ny + 1] = jnp.zeros(ebuf.shape[:1] + ebuf.shape[2:], F32)
@@ -86,48 +93,79 @@
     lane8, row8 = iota((8, Z), 1), iota((8, Z), 0)
     take_ends = (((row8 == 0) & (lane8 == Z - 1)) | ((row8 == 1) & (lane8 == 0))).astype(F32)
 
-    def faces(e, f, n):
+    def copy_to(src, dst, ssem, rsem, to):
+        return pltpu.make_async_remote_copy(src_ref=src, dst_ref=dst, send_sem=ssem, recv_sem=rsem, device_id=to,
+                                            device_id_type=MESH)
+
+    def faces(e, f, n, axis):
         k = n // 2
         out = []
         for side, d in ((0, 1), (1, -1)):
-            def copy(src, dst, ssem, rsem, to):
-                return pltpu.make_async_remote_copy(src_ref=src, dst_ref=dst, send_sem=ssem, recv_sem=rsem,
-                                                    device_id=to, device_id_type=MESH)
-            out.append((copy(zs.at[side, e, pl.ds(0, k)], zr.at[side, e, pl.ds(0, k)], z_send.at[side, e],
-                             z_recv.at[side, e], at(dz=d)),
-                        (gz + d >= 0) & (gz + d < nz), (gz - d >= 0) & (gz - d < nz)))
-            out.append((copy(ys.at[side, e, :, pl.ds(0, n)], yr.at[side, e, :, pl.ds(0, n)], y_send.at[side, e],
-                             y_recv.at[side, e], at(dy=d)),
-                        (gy + d >= 0) & (gy + d < ny), (gy - d >= 0) & (gy - d < ny)))
-            out.append((copy(f.at[:, (n - 1) if side == 0 else 0], xr.at[side, e], x_send.at[side, e],
-                             x_recv.at[side, e], at(dx=d)),
-                        (gx + d >= 0) & (gx + d < nx), (gx - d >= 0) & (gx - d < nx)))
+            if axis == 0:
+                if n == 8:
+                    src, dst = f.at[:, (n - 1) if side == 0 else 0], xr.at[side, e]
+                else:
+                    src, dst = xs.at[side, e, pl.ds(0, n)], xc.at[side, e, pl.ds(0, n)]
+                copy = copy_to(src, dst, x_send.at[side, e], x_recv.at[side, e], at(dx=d))
+                place, count = gx, nx
+            elif axis == 1:
+                copy = copy_to(ys.at[side, e, :, pl.ds(0, n)], yr.at[side, e, :, pl.ds(0, n)], y_send.at[side, e],
+                               y_recv.at[side, e], at(dy=d))
+                place, count = gy, ny
+            else:
+                copy = copy_to(zs.at[side, e, pl.ds(0, k)], zr.at[side, e, pl.ds(0, k)], z_send.at[side, e],
+                               z_recv.at[side, e], at(dz=d))
+                place, count = gz, nz
+            out.append((copy, (place + d >= 0) & (place + d < count), (place - d >= 0) & (place - d < count)))
         return out
 
     sent = []
+
+    def start(e, f, n, axis):
+        for copy, sends, _ in faces(e, f, n, axis):
+            sent.append((copy, sends))
+
+            @pl.when(sends)
+            def _():
+                copy.start()
 
     def send(e, f, n):
         k, per = n // 2, 8 // n
+        for side, x in ((0, n - 1), (1, 0)):
+            for v in range(4):
+                if n == 4:
+                    xs[side, e, v] = f[v, x, pl.ds(0, 8, stride=2), :]
+                elif n == 2:
+                    xs[side, e, v // 2, 4 * (v % 2):4 * (v % 2) + 4] = f[v, x, pl.ds(0, 4, stride=4), :]
+        start(e, f, n, 0)
+        ys[0, e, :, 0:n] = f[:, :, Y - 1:Y, :]
+        ys[1, e, :, 0:n] = f[:, :, 0:1, :]
+        start(e, f, n, 1)
         for c in range(k):
             rows = f[c * per:(c + 1) * per].reshape(128, Z)
             ends = lax.dot_general(take_ends, rows, (((1,), (1,)), ((), ())), precision=HIGH,
                                    preferred_element_type=F32)
             zs[0, e, c] = ends[0:1]
             zs[1, e, c] = ends[1:2]
-        ys[0, e, :, 0:n] = f[:, :, Y - 1:Y, :]
-        ys[1, e, :, 0:n] = f[:, :, 0:1, :]
-        for copy, sends, _ in faces(e, f, n):
-            sent.append((copy, sends))
-
-            @pl.when(sends)
-            def _():
-                copy.start()
+        start(e, f, n, 2)
 
     def receive(e, f, n):
-        for copy, _, receives in faces(e, f, n):
-            @pl.when(receives)
-            def _():
-                copy.wait_recv()
+        for axis in range(3):
+            for copy, _, receives in faces(e, f, n, axis):
+                @pl.when(receives)
+                def _():
+                    copy.wait_recv()
+        if n < 8:
+            for side in range(2):
+                for v in range(4):
+                    if n == 4:
+                        half = xc[side, e, v]
+                        for i in range(2):
+                            xr[side, e, v, pl.ds(i, 8, stride=2), :] = half
+                    else:
+                        half = xc[side, e, v // 2, 4 * (v % 2):4 * (v % 2) + 4]
+                        for i in range(4):
+                            xr[side, e, v, pl.ds(i, 4, stride=4), :] = half
 
     def along_yz(e, f, n, s, c):
         per = 8 // n
@@ -136,6 +174,10 @@
         row, lane = iota(shape, 2), iota(shape, 3)
         lo, hi = (yr[side, e, c * per:(c + 1) * per, 0:n] for side in (0, 1))
         total = jnp.where(row >= s, roll(x, s, 2), lo) + jnp.where(row < Y - s, roll(x, Y - s, 2), hi)
+        if e == C2:
+            out = beyond[c * per:(c + 1) * per]
+            return x, (total + jnp.where(lane >= s, roll(x, s, 3), roll(out, s, 3))
+                       + jnp.where(lane < Z - s, roll(x, Z - s, 3), roll(out, Z - s, 3)))
         total = total + jnp.where(lane >= s, roll(x, s, 3), 0.0) + jnp.where(lane < Z - s, roll(x, Z - s, 3), 0.0)
         ends = jnp.where(row8 == 0, zr[0, e, c], jnp.where(row8 == 1, zr[1, e, c], 0.0))
         put = (((row8 == 0) & (lane8 < s)) | ((row8 == 1) & (lane8 >= Z - s))).astype(F32)
@@ -171,7 +213,6 @@
             put(part, coarsen(b[part] - c_hat * (6.0 * x - near), s))
 
     def corrected(e, coarse, third, out, n, s):
-        receive(e, coarse, n)
         per = 8 // n
         for c in range(n // 2):
             part = slice(c * per, (c + 1) * per)
@@ -189,16 +230,11 @@
             src_ref=row_s.at[k], dst_ref=row_r.at[k, gx], send_sem=ax_send.at[k, d - 1], recv_sem=ax_recv.at[k, d - 1],
             device_id=at(dx=d), device_id_type=MESH) for d in range(1, nx)]
 
-    def plane_copies(k):
-        return [pltpu.make_async_remote_copy(
-            src_ref=plane.at[k, gy], dst_ref=plane.at[k, gy], send_sem=ay_send.at[k, d - 1],
-            recv_sem=ay_recv.at[k, d - 1], device_id=at(dy=d), device_id_type=MESH) for d in range(1, ny)]
+    slabs = [(dy, dz) for dz in (0, -1, 1, -2, 2) for dy in range(ny) if dy or dz]
 
     def deep_copies(k):
-        return [(pltpu.make_async_remote_copy(
-            src_ref=plane.at[k], dst_ref=zb.at[k, 2 - d], send_sem=az_send.at[k, i], recv_sem=az_recv.at[k, i],
-            device_id=at(dz=d), device_id_type=MESH), (gz + d >= 0) & (gz + d < nz), (gz - d >= 0) & (gz - d < nz))
-            for i, d in enumerate((-2, -1, 1, 2))]
+        return [(copy_to(line_b.at[k], zb.at[k, 2 - dz, gy], az_send.at[k, i], az_recv.at[k, i], at(dy=dy, dz=dz)),
+                 (gz + dz >= 0) & (gz + dz < nz), (gz - dz >= 0) & (gz - dz < nz)) for i, (dy, dz) in enumerate(slabs)]
 
     def start_line(k, row):
         row_s[k] = row
@@ -206,21 +242,15 @@
         for copy in line_copies(k):
             copy.start()
 
-    def start_plane(k):
+    def start_deep(k):
         for copy in line_copies(k):
             copy.wait()
-        plane[k, gy] = row_r[k].reshape(nx, Z)
-        for copy in plane_copies(k):
-            copy.start()
-
-    def start_deep(k):
-        for copy in plane_copies(k):
-            copy.wait()
+        line_b[k] = row_r[k].reshape(nx, Z)
         for copy, sends, _ in deep_copies(k):
             @pl.when(sends)
             def _():
                 copy.start()
-        zb[k, 2] = plane[k]
+        zb[k, 2, gy] = line_b[k]
 
     def finish_deep(k):
         for copy, _, receives in deep_copies(k):
@@ -255,8 +285,7 @@
     c2[...] = coarsen(c1[...], 2)
     c3 = coarsen(c2[...], 4)
 
-    total_devices = (nx - 1) + (ny - 1) + (nz - 1)
-    pl.semaphore_wait(barrier, total_devices)
+    pl.semaphore_wait(barrier, partners)
     send(G0, g0, 8)
 
     loads[2].wait()
@@ -282,7 +311,7 @@
 
     second_sweep(G0, g0, v0, 8, 1)
     send(V0, v0, 8)
-    start_plane(0)
+    start_deep(0)
 
     def put_b1(part, r):
         b1[part] = r
@@ -290,8 +319,8 @@
     scale1 = (4.0 * KS) / c1[...]
     residual(V0, inc, c_fine, g0, v0, s0, 8, 1, put_b1)
     send(G1, g1, 4)
-    start_deep(0)
-    gram_line = jnp.sum(plane[0].reshape(ny * nx, Z), axis=0, keepdims=True)
+    finish_deep(0)
+    gram_line = jnp.sum(zb[0, 2].reshape(ny * nx, Z), axis=0, keepdims=True)
     gz_s[...] = gram_line
     gz_r[gz] = gram_line
     gram_copies = [pltpu.make_async_remote_copy(
@@ -314,13 +343,13 @@
     held = []
     residual(V2, b2, 0.0625 * c2[...], g2, v2, s2, 2, 4, lambda part, r: held.append(r))
     start_line(1, to_row(held[0].reshape(8, 8, Z)))
+    send(T2, s2, 2)
 
     shape = (ny, nx, Z)
     lanes = iota(shape, 2)
     place = (gz - 2) * 16 + lanes
     inside = (place >= 0) & (place < nz * 16) & (lanes < 80)
     km = jnp.where(inside, KS, 0.0)
-    finish_deep(0)
     c3g = [jnp.where(inside, spread(0, q), 1.0) for q in range(2)]
     for q in range(2):
         cc3[q] = (1.0 / 64) * c3g[q]
@@ -336,7 +365,7 @@
     c5g = coarsen_gathered(halved[:, 0] + halved[:, 1], 2)
     inv5[...] = jnp.where(inside[:ny // 2], (1024.0 * KS) / c5g, 0.0)
 
-    start_plane(1)
+    start_deep(1)
 
     for copy in gram_copies:
         copy.wait()
@@ -382,10 +411,7 @@
             rem = [prev[j, x, part] - sum(proj_w[m][j] * vo[m] for m in range(4)) for j in range(4)]
             for j in range(4):
                 ortho[j, x, part] = sum(inv_w[j][i] * rem[i] for i in range(j + 1))
-    outs = [pltpu.make_async_copy(ortho, ortho_hbm, out_sem.at[0])]
-    outs[0].start()
-
-    start_deep(1)
+
     finish_deep(1)
 
     rows_i = iota(shape, 1)
@@ -430,48 +456,67 @@
             v5 = 0.2 * v5 + g5 + km5 * near_coarse(v5, 4)
         p4 = jnp.stack([v5, v5], axis=1).reshape(ny, nx, Z)
         e4 = third4 + 0.2 * p4 + km * near_coarse(p4, 2)
-        xz = along_xz(e4, 1) + 1.2 / 6.0 * 0.0
+        xz = along_xz(e4, 1)
         ebuf[2 * vec, 1:ny + 1, 8:8 + nx] = third[0] + 0.2 * e4 + km * (xz + e4 + down(e4))
         ebuf[2 * vec + 1, 1:ny + 1, 8:8 + nx] = third[1] + 0.2 * e4 + km * (xz + e4 + up(e4))
 
-    def cells(dy, dx):
-        return ebuf[:, gy + 1 + dy, pl.ds(8 + gx + dx, 1), :].reshape(8, Z)
+    receive(T2, s2, 2)
+    around = [(dx, dy) for dx in (-1, 0, 1) for dy in (0, -1, 1)]
+    stacked = jnp.concatenate([ebuf[:, gy + 1 + dy, pl.ds(8 + gx + dx, 1), :].reshape(8, Z) for dx, dy in around], axis=0)
     li, lj = iota((Z, Z), 0), iota((Z, Z), 1)
-    widen = (li == 32 + lj // 8).astype(F32)
-    beside = ((li == 31 + (lj + 4) // 8) | (li == 32 + (lj + 4) // 8)).astype(F32)
-    own = cells(0, 0)
-    stacked = jnp.concatenate([own, cells(0, -1), cells(0, 1), cells(-1, 0), cells(1, 0)], axis=0)
-    wide_rows = lax.dot_general(stacked, widen, (((1,), (0,)), ((), ())), precision=HIGH, preferred_element_type=F32)
-    z_rows = lax.dot_general(own, beside, (((1,), (0,)), ((), ())), precision=HIGH, preferred_element_type=F32)
+    after = lj < 64
+    maps = [li == 32 + lj // 8, (li == 31 + (lj + 4) // 8) | (li == 32 + (lj + 4) // 8),
+            li == jnp.where(after, 48, 31), (li == jnp.where(after, 47, 31)) | (li == jnp.where(after, 48, 32))]
+    spread_rows = [lax.dot_general(stacked, m.astype(F32), (((1,), (0,)), ((), ())), precision=HIGH,
+                                   preferred_element_type=F32) for m in maps]
+
+    def cell(kind, vec, y2, dx, dy=0):
+        i = 8 * around.index((dx, dy)) + 2 * vec + y2
+        return wide(spread_rows[kind][i:i + 1])
+
+    def flag(cond):
+        return jnp.where(cond, 1.0, 0.0).astype(F32)
+    x_in, y_in = (flag(gx > 0), flag(gx < nx - 1)), (flag(gy > 0), flag(gy < ny - 1))
+    z_in = jnp.where(lane8 < 64, flag(gz < nz - 1), flag(gz > 0))
+    ends = jnp.where(row8 == 0, zr[0, T2, 0], jnp.where(row8 == 1, zr[1, T2, 0], 0.0))
+    put = (((row8 == 0) & (lane8 >= 64)) | ((row8 == 1) & (lane8 < 64))).astype(F32)
+    third_out = lax.dot_general(ends, put, (((0,), (0,)), ((), ())), precision=HIGH, preferred_element_type=F32)
+    third_out = third_out.reshape(4, 2, Y, Z)
     for vec in range(4):
-        q = [2 * vec, 2 * vec + 1]
-        a = [wide(wide_rows[i:i + 1]) for i in q]
-        x_lo = [wide(wide_rows[8 + i:9 + i]) for i in q]
-        x_hi = [wide(wide_rows[16 + i:17 + i]) for i in q]
-        y_lo = wide(wide_rows[24 + q[1]:25 + q[1]])
-        y_hi = wide(wide_rows[32 + q[0]:33 + q[0]])
-        z_sum = [wide(z_rows[i:i + 1]) for i in q]
-        mid = a[0] + a[1]
-        y_sum = [jnp.where(row8 < 4, y_lo + a[0], mid), jnp.where(row8 < 4, mid, a[1] + y_hi)]
-        for h in range(2):
-            part = slice(8 * h, 8 * h + 8)
-            base = 0.2 * a[h] + KS * (y_sum[h] + z_sum[h] + a[h])
-            e2[vec, 0, part] = s2[vec, 0, part] + base + KS * x_lo[h]
-            e2[vec, 1, part] = s2[vec, 1, part] + base + KS * x_hi[h]
-
-    send(C2, e2, 2)
+        for dx, others in ((0, (-1, 1)), (-1, (0,)), (1, (0,))):
+            for kind in (0, 2) if dx == 0 else (0,):
+                a = [cell(kind, vec, y2, dx) for y2 in range(2)]
+                mid = a[0] + a[1]
+                y_sum = [jnp.where(row8 < 4, cell(kind, vec, 1, dx, -1) + a[0], mid),
+                         jnp.where(row8 < 4, mid, a[1] + cell(kind, vec, 0, dx, 1))]
+                for h in range(2):
+                    part = slice(8 * h, 8 * h + 8)
+                    base = 0.2 * a[h] + KS * (y_sum[h] + cell(kind + 1, vec, h, dx) + a[h])
+                    for x, other in enumerate(others):
+                        value = base + KS * cell(kind, vec, h, other)
+                        if dx:
+                            side = 0 if dx < 0 else 1
+                            xr[side, C2, vec, part] = xr[side, T2, vec, part] + x_in[side] * value
+                        elif kind == 0:
+                            e2[vec, x, part] = s2[vec, x, part] + value
+                        else:
+                            beyond[vec, x, part] = third_out[vec, x, part] + z_in * value
+        for side, dy, y2 in ((0, -1, 1), (1, 1, 0)):
+            b = cell(0, vec, y2, 0, dy)[0:1]
+            base = 0.2 * b + KS * (2.0 * b + cell(0, vec, 1 - y2, 0)[0:1] + cell(1, vec, y2, 0, dy)[0:1])
+            for x, dx in enumerate((-1, 1)):
+                value = base + KS * cell(0, vec, y2, dx, dy)[0:1]
+                yr[side, C2, vec, x] = yr[side, T2, vec, x] + y_in[side] * value
+
     corrected(C2, e2, s1, e1, 2, 2)
     send(C1, e1, 4)
+    receive(C1, e1, 4)
     corrected(C1, e1, s0, e0, 4, 1)
     send(C0, e0, 8)
-    outs.append(pltpu.make_async_copy(e0, prec_hbm, out_sem.at[1]))
-    outs[1].start()
     receive(C0, e0, 8)
     for c in range(4):
         x, near = neighbours(C0, e0, 8, 1, c)
         oper[c:c + 1] = c_fine * (6.0 * x - near)
-    outs.append(pltpu.make_async_copy(oper, oper_hbm, out_sem.at[2]))
-    outs[2].start()
     for copy, sends in sent:
         @pl.when(sends)
         def _():
@@ -481,8 +526,15 @@
             @pl.when(sends)
             def _():
                 copy.wait_send()
-    for out in outs:
-        out.wait()
+
+
+def write_out(*refs):
+    sems = refs[-1]
+    copies = [pltpu.make_async_copy(refs[i], refs[5 + i], sems.at[i]) for i in range(5)]
+    for copy in copies:
+        copy.start()
+    for copy in copies:
+        copy.wait()
 
 
 def per_device(shape, old_basis, previous, incoming, coefficient):
@@ -494,27 +546,35 @@
     vm = lambda *s: pltpu.VMEM(s, F32)
     whole = jax.ShapeDtypeStruct((4, 8, 16, 128), F32)
     small = jax.ShapeDtypeStruct((4, 4), F32)
+    held = (vm(4, 8, 16, 128), vm(4, 4), vm(4, 4), vm(4, 8, 16, 128), vm(4, 8, 16, 128))
     any_spec = pl.BlockSpec(memory_space=pl.ANY)
     vmem_spec = pl.BlockSpec(memory_space=pltpu.VMEM)
-    return pl.pallas_call(
+    results = pl.pallas_call(
         functools.partial(kernel, nx, ny, nz),
-        out_shape=(whole, small, small, whole, whole),
+        out_shape=held,
         in_specs=[any_spec] * 4,
-        out_specs=(any_spec, vmem_spec, vmem_spec, any_spec, any_spec),
+        out_specs=(vmem_spec,) * 5,
         scratch_shapes=[
-            big, big, big, vm(8, 16, 128), big, big,
-            big, big, big, mid, mid, mid, mid, low, low, low, low, low, mid, big, vm(4, 16, 128), vm(2, 16, 128),
-            vm(2, 9, 4, 16, 128), vm(2, 9, 4, 8, 1, 128), vm(2, 9, 4, 8, 1, 128),
-            vm(2, 9, 4, 1, 128), vm(2, 9, 4, 1, 128),
-            vm(2, 1, 128), vm(2, nx, 1, 128), vm(2, ny, nx, 128), vm(2, 5, ny, nx, 128), vm(1, 128), vm(nz, 1, 128),
+            big, big, big, vm(8, 16, 128),
+            big, big, big, mid, mid, mid, mid, low, low, low, low, low, mid, vm(4, 16, 128), vm(2, 16, 128), low,
+            vm(2, 9, 4, 8, 128), vm(2, 9, 4, 8, 128), vm(2, 10, 4, 16, 128), vm(2, 9, 4, 8, 1, 128),
+            vm(2, 10, 4, 8, 1, 128), vm(2, 9, 4, 1, 128), vm(2, 9, 4, 1, 128),
+            vm(2, 1, 128), vm(2, nx, 1, 128), vm(2, nx, 128), vm(2, 5, ny, nx, 128), vm(1, 128), vm(nz, 1, 128),
             vm(2, ny, nx, 128), vm(2, ny, nx, 128), vm(ny, nx, 128), vm(ny, nx, 128), vm(ny // 2, nx, 128),
             vm(8, ny + 2, nx + 16, 128),
-            dma((4,)), dma((3,)), dma((2, 9)), dma((2, 9)), dma((2, 9)), dma((2, 9)), dma((2, 9)), dma((2, 9)),
-            dma((2, nx - 1)), dma((2, nx - 1)), dma((2, ny - 1)), dma((2, ny - 1)), dma((2, 4)), dma((2, 4)),
+            dma((4,)), dma((2, 9)), dma((2, 9)), dma((2, 9)), dma((2, 9)), dma((2, 9)), dma((2, 9)),
+            dma((2, nx - 1)), dma((2, nx - 1)), dma((2, 5 * ny - 1)), dma((2, 5 * ny - 1)),
             dma((nz - 1,)), dma((nz - 1,)),
         ],
         compiler_params=pltpu.CompilerParams(collective_id=0, has_side_effects=True),
     )(old_basis, previous, incoming, coefficient)
+    return pl.pallas_call(
+        write_out,
+        out_shape=(whole, small, small, whole, whole),
+        in_specs=[vmem_spec] * 5,
+        out_specs=(any_spec,) * 5,
+        scratch_shapes=[dma((5,))],
+    )(*[pltpu.with_memory_space_constraint(r, pltpu.VMEM) for r in results])
 
 
 def solution(mesh):

time: 81.7 us -> 72.2 us (0.88)
  local copies, waits for them, and re-layouts: 4.73 us -> 0 us
  Pallas kernels: 76.1 us -> 71.4 us
    unnamed x13 -> x0, local copies, waits for them, and re-layouts: 4.73 us -> none
    pallas_call x1 -> x2, Pallas kernels: 76.1 us -> 71.4 us  [the longest x1 70.5 us: per_device(): pl.pallas_call(functools.partial(kernel, nx, ny, nz), out_shape=held, in_...]
where the time goes in v2:
time: 72.2 us; the launch traced here: 72 us
  Pallas kernels  71.4 us (99%)
    pallas_call x1, Pallas kernels, per_device(): pl.pallas_call(functools.partial(kernel, nx, ny, nz), out_shape=held, in_...  70.5 us

profile of v2, /device:TPU:1, one launch (start us, length us, event | category | flops | bytes accessed | tf_op | source)
XLA Modules:
  0.0 72.0 jit_solution(12463199381835872237)
XLA Ops:
  0.6 70.5 %shard_map.83 = (f32[4,8,16,128]{3,2,1,0:T(8,128)S(1)}, f32[4,4]{1,0:T(4,128)S(1)}, f32[4,4]{1,0:T(4,128)S(1)}, f32[4,8,16,128]{3,2,1,0:T(8,128)S(1)}, f32[4,8,16,128]{3,2,1,0:T(8,128)S(1)}) custom-call(f32[4,8,16,128]{3,2,1,0:T(8,128)} %old_hbm.1, f32[4,8,16,128]{3,2,1,0:T(8,128)} %prev_hbm.1, f32[4,8,16,128]{3,2,1,0:T(8,128)} %inc_hbm.1, ...), custom_call_target="tpu_custom_call" | custom-call | tf_op jit(solution)/shard_map/pallas_call | solution.py:552
  71.1 0.9 %shard_map.84 = (f32[4,8,16,128]{3,2,1,0:T(8,128)}, f32[4,4]{1,0:T(4,128)}, f32[4,4]{1,0:T(4,128)}, f32[4,8,16,128]{3,2,1,0:T(8,128)}, f32[4,8,16,128]{3,2,1,0:T(8,128)}) custom-call(f32[4,8,16,128]{3,2,1,0:T(8,128)S(1)} %get-tuple-element.10.refs_0_, f32[4,4]{1,0:T(4,128)S(1)} %get-tuple-element.11.refs_1_, f32[4,4]{1,0:T(4,128)S(1)} %get-tuple-element.12.refs_2_, ...), custom_call_target="tpu_custom_call" | custom-call | tf_op jit(solution)/shard_map/pallas_call | solution.py:571

commit v3 on v2

--- a/solution.py
+++ b/solution.py
@@ -43,7 +43,7 @@
            ortho, proj_ref, tri_ref, e0, oper,
            old, prev, inc, coef,
            g0, v0, s0, b1, g1, v1, s1, b2, g2, v2, s2, e2, e1, c1, c2, beyond,
-           xs, xc, xr, ys, yr, zs, zr, row_s, row_r, line_b, zb, gz_s, gz_r,
+           xs, xc, xr, ys, yr, zs, zr, row_s, row_r, line_b, zb, planes, passed, all_planes,
            cc3, inv3, cc4, inv4, inv5, ebuf,
            in_sem, x_send, x_recv, y_send, y_recv, z_send, z_recv,
            ax_send, ax_recv, az_send, az_recv, ag_send, ag_recv):
@@ -60,45 +60,26 @@
     for load in loads:
         load.start()
 
-    for cond, buf, side in ((gx == 0, xr, 0), (gx == nx - 1, xr, 1), (gx == 0, xc, 0), (gx == nx - 1, xc, 1), (gy == 0, yr, 0), (gy == ny - 1, yr, 1),
-                            (gz == 0, zr, 0), (gz == nz - 1, zr, 1)):
-        @pl.when(cond)
-        def _():
-            buf[side] = jnp.zeros(buf.shape[1:], F32)
-    for d in (-2, -1, 1, 2):
-        @pl.when((gz + d < 0) | (gz + d >= nz))
-        def _():
-            zb[:, 2 + d] = jnp.zeros((2,) + zb.shape[2:], F32)
-
     barrier = pltpu.get_barrier_semaphore()
     for d in range(1, nx):
         pl.semaphore_signal(barrier, inc=1, device_id=at(dx=d), device_id_type=MESH)
-    for d in range(1, nz):
-        pl.semaphore_signal(barrier, inc=1, device_id=at(dz=d), device_id_type=MESH)
-    partners = jnp.int32(nx - 1 + nz - 1)
+    partners = jnp.int32(nx - 1)
     for dz in range(-2, 3):
         reach = (gz + dz >= 0) & (gz + dz < nz)
-        partners = partners + jnp.where(reach, ny - 1, 0)
+        partners = partners + jnp.where(reach, ny - (dz == 0), 0)
 
         @pl.when(reach)
         def _():
-            for dy in range(1, ny):
+            for dy in range(1 if dz == 0 else 0, ny):
                 pl.semaphore_signal(barrier, inc=1, device_id=at(dy=dy, dz=dz), device_id_type=MESH)
 
-    ebuf[:, 0] = jnp.zeros(ebuf.shape[:1] + ebuf.shape[2:], F32)
-    ebuf[:, ny + 1] = jnp.zeros(ebuf.shape[:1] + ebuf.shape[2:], F32)
-    ebuf[:, 1:ny + 1, 0:8] = jnp.zeros((8, ny, 8, Z), F32)
-    ebuf[:, 1:ny + 1, 8 + nx:] = jnp.zeros((8, ny, 8, Z), F32)
-
     lane8, row8 = iota((8, Z), 1), iota((8, Z), 0)
-    take_ends = (((row8 == 0) & (lane8 == Z - 1)) | ((row8 == 1) & (lane8 == 0))).astype(F32)
-
+    wide = lambda a: jnp.broadcast_to(a, (8, Z))
     def copy_to(src, dst, ssem, rsem, to):
         return pltpu.make_async_remote_copy(src_ref=src, dst_ref=dst, send_sem=ssem, recv_sem=rsem, device_id=to,
                                             device_id_type=MESH)
 
     def faces(e, f, n, axis):
-        k = n // 2
         out = []
         for side, d in ((0, 1), (1, -1)):
             if axis == 0:
@@ -113,7 +94,7 @@
                                y_recv.at[side, e], at(dy=d))
                 place, count = gy, ny
             else:
-                copy = copy_to(zs.at[side, e, pl.ds(0, k)], zr.at[side, e, pl.ds(0, k)], z_send.at[side, e],
+                copy = copy_to(zs.at[side, e], zr.at[side, e], z_send.at[side, e],
                                z_recv.at[side, e], at(dz=d))
                 place, count = gz, nz
             out.append((copy, (place + d >= 0) & (place + d < count), (place - d >= 0) & (place - d < count)))
@@ -130,7 +111,6 @@
                 copy.start()
 
     def send(e, f, n):
-        k, per = n // 2, 8 // n
         for side, x in ((0, n - 1), (1, 0)):
             for v in range(4):
                 if n == 4:
@@ -141,12 +121,13 @@
         ys[0, e, :, 0:n] = f[:, :, Y - 1:Y, :]
         ys[1, e, :, 0:n] = f[:, :, 0:1, :]
         start(e, f, n, 1)
-        for c in range(k):
-            rows = f[c * per:(c + 1) * per].reshape(128, Z)
-            ends = lax.dot_general(take_ends, rows, (((1,), (1,)), ((), ())), precision=HIGH,
-                                   preferred_element_type=F32)
-            zs[0, e, c] = ends[0:1]
-            zs[1, e, c] = ends[1:2]
+        packed = [jnp.zeros((8, Z), F32)] * 2
+        for i in range(8 * n):
+            tile = f[i // (2 * n), i // 2 % n, 8 * (i % 2):8 * (i % 2) + 8]
+            here = lane8 == i
+            packed = [jnp.where(here, tile[:, x:x + 1], p) for x, p in zip((Z - 1, 0), packed)]
+        zs[0, e] = packed[0]
+        zs[1, e] = packed[1]
         start(e, f, n, 2)
 
     def receive(e, f, n):
@@ -167,6 +148,10 @@
                         for i in range(4):
                             xr[side, e, v, pl.ds(i, 4, stride=4), :] = half
 
+    def z_halo(e, side, first, count):
+        packed = zr[side, e]
+        return jnp.concatenate([jnp.broadcast_to(packed[:, i:i + 1], (8, Z)) for i in range(first, first + count)], axis=0)
+
     def along_yz(e, f, n, s, c):
         per = 8 // n
         shape = (per, n, Y, Z)
@@ -178,11 +163,9 @@
             out = beyond[c * per:(c + 1) * per]
             return x, (total + jnp.where(lane >= s, roll(x, s, 3), roll(out, s, 3))
                        + jnp.where(lane < Z - s, roll(x, Z - s, 3), roll(out, Z - s, 3)))
-        total = total + jnp.where(lane >= s, roll(x, s, 3), 0.0) + jnp.where(lane < Z - s, roll(x, Z - s, 3), 0.0)
-        ends = jnp.where(row8 == 0, zr[0, e, c], jnp.where(row8 == 1, zr[1, e, c], 0.0))
-        put = (((row8 == 0) & (lane8 < s)) | ((row8 == 1) & (lane8 >= Z - s))).astype(F32)
-        halo = lax.dot_general(ends, put, (((0,), (0,)), ((), ())), precision=HIGH, preferred_element_type=F32)
-        return x, total + halo.reshape(shape)
+        lo, hi = (z_halo(e, side, 16 * c, 16).reshape(shape) for side in (0, 1))
+        return x, (total + jnp.where(lane >= s, roll(x, s, 3), lo)
+                   + jnp.where(lane < Z - s, roll(x, Z - s, 3), hi))
 
     def x_ends(e, n, c):
         per = 8 // n
@@ -258,6 +241,40 @@
             def _():
                 copy.wait_recv()
 
+    rounds = (nz - 2) // 2
+
+    def chain_copies(i):
+        out = []
+        for side, d in ((0, 2), (1, -2)):
+            src = planes.at[pl.ds(0 if side == 0 else 3, 2)] if i == 0 else passed.at[side, i - 1]
+            copy = copy_to(src, passed.at[side, i], ag_send.at[side, i], ag_recv.at[side, i], at(dz=d))
+            near_row = 3 + 2 * i
+            if side == 0:
+                out.append((copy, (gz + d < nz) & (gz + d - near_row >= 0), gz - near_row >= 0))
+            else:
+                out.append((copy, (gz + d >= 0) & (gz + d + near_row < nz), gz + near_row < nz))
+        return out
+
+    def chain_start(i):
+        if i >= rounds:
+            return
+        for copy, sends, _ in chain_copies(i):
+            @pl.when(sends)
+            def _():
+                copy.start()
+
+    def chain_wait(i):
+        if i >= rounds:
+            return
+        for copy, _, receives in chain_copies(i):
+            @pl.when(receives)
+            def _():
+                copy.wait_recv()
+
+    def chain_next(i):
+        chain_wait(i - 1)
+        chain_start(i)
+
     def to_row(blocks):
         q = blocks.shape[0]
         rows = jnp.zeros((8, Z), F32)
@@ -281,12 +298,34 @@
     scale = KS / c_fine
     for v in range(4):
         g0[v] = inc[v] * scale
+    pl.semaphore_wait(barrier, partners)
+    send(G0, g0, 8)
+    for cond, buf, side in ((gx == 0, xr, 0), (gx == nx - 1, xr, 1), (gx == 0, xc, 0), (gx == nx - 1, xc, 1), (gy == 0, yr, 0), (gy == ny - 1, yr, 1),
+                            (gz == 0, zr, 0), (gz == nz - 1, zr, 1)):
+        @pl.when(cond)
+        def _():
+            buf[side] = jnp.zeros(buf.shape[1:], F32)
+    for side in range(2):
+        for i in range((nz - 2) // 2):
+            missing = (gz - 3 - 2 * i < 0) if side == 0 else (gz + 3 + 2 * i >= nz)
+
+            @pl.when(missing)
+            def _():
+                passed[side, i] = jnp.zeros(passed.shape[2:], F32)
+    for d in (-2, -1, 1, 2):
+        @pl.when((gz + d < 0) | (gz + d >= nz))
+        def _():
+            zb[:, 2 + d] = jnp.zeros((2,) + zb.shape[2:], F32)
+
+    ebuf[:, 0] = jnp.zeros(ebuf.shape[:1] + ebuf.shape[2:], F32)
+    ebuf[:, ny + 1] = jnp.zeros(ebuf.shape[:1] + ebuf.shape[2:], F32)
+    ebuf[:, 1:ny + 1, 0:8] = jnp.zeros((8, ny, 8, Z), F32)
+    ebuf[:, 1:ny + 1, 8 + nx:] = jnp.zeros((8, ny, 8, Z), F32)
+
     c1[...] = coarsen(c_fine, 1)
     c2[...] = coarsen(c1[...], 2)
     c3 = coarsen(c2[...], 4)
 
-    pl.semaphore_wait(barrier, partners)
-    send(G0, g0, 8)
 
     loads[2].wait()
     loads[3].wait()
@@ -319,15 +358,6 @@
     scale1 = (4.0 * KS) / c1[...]
     residual(V0, inc, c_fine, g0, v0, s0, 8, 1, put_b1)
     send(G1, g1, 4)
-    finish_deep(0)
-    gram_line = jnp.sum(zb[0, 2].reshape(ny * nx, Z), axis=0, keepdims=True)
-    gz_s[...] = gram_line
-    gz_r[gz] = gram_line
-    gram_copies = [pltpu.make_async_remote_copy(
-        src_ref=gz_s, dst_ref=gz_r.at[gz], send_sem=ag_send.at[d - 1], recv_sem=ag_recv.at[d - 1],
-        device_id=at(dz=d), device_id_type=MESH) for d in range(1, nz)]
-    for copy in gram_copies:
-        copy.start()
 
     second_sweep(G1, g1, v1, 4, 2)
     send(V1, v1, 4)
@@ -338,12 +368,18 @@
         g2[part] = r * scale2
     residual(V1, b1, 0.25 * c1[...], g1, v1, s1, 4, 2, put_b2)
     send(G2, g2, 2)
+    finish_deep(0)
+    for i in range(5):
+        planes[i] = jnp.sum(zb[0, i].reshape(ny * nx, Z), axis=0, keepdims=True)
+    chain_start(0)
     second_sweep(G2, g2, v2, 2, 4)
     send(V2, v2, 2)
+    chain_next(1)
     held = []
     residual(V2, b2, 0.0625 * c2[...], g2, v2, s2, 2, 4, lambda part, r: held.append(r))
     start_line(1, to_row(held[0].reshape(8, 8, Z)))
     send(T2, s2, 2)
+    chain_next(2)
 
     shape = (ny, nx, Z)
     lanes = iota(shape, 2)
@@ -367,9 +403,117 @@
 
     start_deep(1)
 
-    for copy in gram_copies:
-        copy.wait()
-    line = jnp.sum(gz_r[...].reshape(nz, Z), axis=0, keepdims=True)
+    chain_next(3)
+    finish_deep(1)
+    chain_next(4)
+
+    rows_i = iota(shape, 1)
+    zero = jnp.zeros((1, nx, Z), F32)
+
+    def along_xz(v, s):
+        r = rows_i[:v.shape[0]]
+        out = jnp.where(r >= s, roll(v, s, 1), 0.0) + jnp.where(r < nx - s, roll(v, nx - s, 1), 0.0)
+        return out + roll(v, s, 2) + roll(v, Z - s, 2)
+
+    def up(v):
+        return zero if v.shape[0] == 1 else jnp.concatenate([v[1:], zero], axis=0)
+
+    def down(v):
+        return zero if v.shape[0] == 1 else jnp.concatenate([zero, v[:-1]], axis=0)
+
+    def near3(v):
+        return [along_xz(v[0], 1) + v[1] + down(v[1]), along_xz(v[1], 1) + v[0] + up(v[0])]
+
+    def near_coarse(v, s):
+        return along_xz(v, s) + up(v) + down(v)
+
+    km5 = km[:ny // 2]
+    for vec in range(4):
+        b = [spread(1, 2 * vec + q) for q in range(2)]
+        g = [b[q] * inv3[q] for q in range(2)]
+        near = near3(g)
+        v = [1.2 * g[q] + km * near[q] for q in range(2)]
+        near = near3(v)
+        third = [0.2 * v[q] + g[q] + km * near[q] for q in range(2)]
+        r = [b[q] - cc3[q] * (6.0 * v[q] - near[q]) for q in range(2)]
+        b4 = coarsen_gathered(jnp.where(inside, r[0] + r[1], 0.0), 1)
+        g4 = b4 * inv4[...]
+        v4 = 1.2 * g4 + km * near_coarse(g4, 2)
+        n4 = near_coarse(v4, 2)
+        third4 = 0.2 * v4 + g4 + km * n4
+        r4_ = b4 - cc4[...] * (6.0 * v4 - n4)
+        r4_ = jnp.where(inside, r4_, 0.0).reshape(ny // 2, 2, nx, Z)
+        g5 = coarsen_gathered(r4_[:, 0] + r4_[:, 1], 2) * inv5[...]
+        v5 = g5
+        for _ in range(3):
+            v5 = 0.2 * v5 + g5 + km5 * near_coarse(v5, 4)
+        p4 = jnp.stack([v5, v5], axis=1).reshape(ny, nx, Z)
+        e4 = third4 + 0.2 * p4 + km * near_coarse(p4, 2)
+        xz = along_xz(e4, 1)
+        ebuf[2 * vec, 1:ny + 1, 8:8 + nx] = third[0] + 0.2 * e4 + km * (xz + e4 + down(e4))
+        ebuf[2 * vec + 1, 1:ny + 1, 8:8 + nx] = third[1] + 0.2 * e4 + km * (xz + e4 + up(e4))
+
+    receive(T2, s2, 2)
+    around = [(dx, dy) for dx in (-1, 0, 1) for dy in (0, -1, 1)]
+    stacked = jnp.concatenate([ebuf[:, gy + 1 + dy, pl.ds(8 + gx + dx, 1), :].reshape(8, Z) for dx, dy in around], axis=0)
+    li, lj = iota((Z, Z), 0), iota((Z, Z), 1)
+    after = lj < 64
+    maps = [li == 32 + lj // 8, (li == 31 + (lj + 4) // 8) | (li == 32 + (lj + 4) // 8),
+            li == jnp.where(after, 48, 31), (li == jnp.where(after, 47, 31)) | (li == jnp.where(after, 48, 32))]
+    spread_rows = [lax.dot_general(stacked, m.astype(F32), (((1,), (0,)), ((), ())), precision=HIGH,
+                                   preferred_element_type=F32) for m in maps]
+
+    def cell(kind, vec, y2, dx, dy=0):
+        i = 8 * around.index((dx, dy)) + 2 * vec + y2
+        return wide(spread_rows[kind][i:i + 1])
+
+    def flag(cond):
+        return jnp.where(cond, 1.0, 0.0).astype(F32)
+    x_in, y_in = (flag(gx > 0), flag(gx < nx - 1)), (flag(gy > 0), flag(gy < ny - 1))
+    z_in = jnp.where(lane8 < 64, flag(gz < nz - 1), flag(gz > 0))
+    third_out = jnp.where(iota((128, Z), 1) < 64, z_halo(T2, 1, 0, 16), z_halo(T2, 0, 0, 16)).reshape(4, 2, Y, Z)
+    for vec in range(4):
+        for dx, others in ((0, (-1, 1)), (-1, (0,)), (1, (0,))):
+            for kind in (0, 2) if dx == 0 else (0,):
+                a = [cell(kind, vec, y2, dx) for y2 in range(2)]
+                mid = a[0] + a[1]
+                y_sum = [jnp.where(row8 < 4, cell(kind, vec, 1, dx, -1) + a[0], mid),
+                         jnp.where(row8 < 4, mid, a[1] + cell(kind, vec, 0, dx, 1))]
+                for h in range(2):
+                    part = slice(8 * h, 8 * h + 8)
+                    base = 0.2 * a[h] + KS * (y_sum[h] + cell(kind + 1, vec, h, dx) + a[h])
+                    for x, other in enumerate(others):
+                        value = base + KS * cell(kind, vec, h, other)
+                        if dx:
+                            side = 0 if dx < 0 else 1
+                            xr[side, C2, vec, part] = xr[side, T2, vec, part] + x_in[side] * value
+                        elif kind == 0:
+                            e2[vec, x, part] = s2[vec, x, part] + value
+                        else:
+                            beyond[vec, x, part] = third_out[vec, x, part] + z_in * value
+        for side, dy, y2 in ((0, -1, 1), (1, 1, 0)):
+            b = cell(0, vec, y2, 0, dy)[0:1]
+            base = 0.2 * b + KS * (2.0 * b + cell(0, vec, 1 - y2, 0)[0:1] + cell(1, vec, y2, 0, dy)[0:1])
+            for x, dx in enumerate((-1, 1)):
+                value = base + KS * cell(0, vec, y2, dx, dy)[0:1]
+                yr[side, C2, vec, x] = yr[side, T2, vec, x] + y_in[side] * value
+
+    corrected(C2, e2, s1, e1, 2, 2)
+    send(C1, e1, 4)
+    chain_next(5)
+    receive(C1, e1, 4)
+    chain_next(6)
+    corrected(C1, e1, s0, e0, 4, 1)
+    send(C0, e0, 8)
+    for i in range(7, rounds + 1):
+        chain_next(i)
+    for i in range(5):
+        all_planes[gz + nz + i - 2] = planes[i]
+    for i in range(rounds):
+        for j in range(2):
+            all_planes[gz + nz - 4 - 2 * i + j] = passed[0, i, j]
+            all_planes[gz + nz + 3 + 2 * i + j] = passed[1, i, j]
+    line = jnp.sum(all_planes[nz:2 * nz].reshape(nz, Z), axis=0, keepdims=True)
     column = jnp.sum(jnp.where(at_lane, line, 0.0), axis=1, keepdims=True)
     column = column * (1.0 / float(nx * ny * nz * X * Y * Z))
     value = {key: column[p:p + 1] for p, key in enumerate(pairs)}
@@ -401,7 +545,6 @@
                 out_t = jnp.where(here, low[j][i], out_t)
     proj_ref[...] = out_p
     tri_ref[...] = out_t
-    wide = lambda a: jnp.broadcast_to(a, (8, Z))
     proj_w = [[wide(a) for a in line_] for line_ in proj]
     inv_w = [[wide(inverse[j][i]) if i <= j else None for i in range(4)] for j in range(4)]
     for x in range(X):
@@ -412,112 +555,17 @@
             for j in range(4):
                 ortho[j, x, part] = sum(inv_w[j][i] * rem[i] for i in range(j + 1))
 
-    finish_deep(1)
-
-    rows_i = iota(shape, 1)
-    zero = jnp.zeros((1, nx, Z), F32)
-
-    def along_xz(v, s):
-        r = rows_i[:v.shape[0]]
-        out = jnp.where(r >= s, roll(v, s, 1), 0.0) + jnp.where(r < nx - s, roll(v, nx - s, 1), 0.0)
-        return out + roll(v, s, 2) + roll(v, Z - s, 2)
-
-    def up(v):
-        return zero if v.shape[0] == 1 else jnp.concatenate([v[1:], zero], axis=0)
-
-    def down(v):
-        return zero if v.shape[0] == 1 else jnp.concatenate([zero, v[:-1]], axis=0)
-
-    def near3(v):
-        return [along_xz(v[0], 1) + v[1] + down(v[1]), along_xz(v[1], 1) + v[0] + up(v[0])]
-
-    def near_coarse(v, s):
-        return along_xz(v, s) + up(v) + down(v)
-
-    km5 = km[:ny // 2]
-    for vec in range(4):
-        b = [spread(1, 2 * vec + q) for q in range(2)]
-        g = [b[q] * inv3[q] for q in range(2)]
-        near = near3(g)
-        v = [1.2 * g[q] + km * near[q] for q in range(2)]
-        near = near3(v)
-        third = [0.2 * v[q] + g[q] + km * near[q] for q in range(2)]
-        r = [b[q] - cc3[q] * (6.0 * v[q] - near[q]) for q in range(2)]
-        b4 = coarsen_gathered(jnp.where(inside, r[0] + r[1], 0.0), 1)
-        g4 = b4 * inv4[...]
-        v4 = 1.2 * g4 + km * near_coarse(g4, 2)
-        n4 = near_coarse(v4, 2)
-        third4 = 0.2 * v4 + g4 + km * n4
-        r4_ = b4 - cc4[...] * (6.0 * v4 - n4)
-        r4_ = jnp.where(inside, r4_, 0.0).reshape(ny // 2, 2, nx, Z)
-        g5 = coarsen_gathered(r4_[:, 0] + r4_[:, 1], 2) * inv5[...]
-        v5 = g5
-        for _ in range(3):
-            v5 = 0.2 * v5 + g5 + km5 * near_coarse(v5, 4)
-        p4 = jnp.stack([v5, v5], axis=1).reshape(ny, nx, Z)
-        e4 = third4 + 0.2 * p4 + km * near_coarse(p4, 2)
-        xz = along_xz(e4, 1)
-        ebuf[2 * vec, 1:ny + 1, 8:8 + nx] = third[0] + 0.2 * e4 + km * (xz + e4 + down(e4))
-        ebuf[2 * vec + 1, 1:ny + 1, 8:8 + nx] = third[1] + 0.2 * e4 + km * (xz + e4 + up(e4))
-
-    receive(T2, s2, 2)
-    around = [(dx, dy) for dx in (-1, 0, 1) for dy in (0, -1, 1)]
-    stacked = jnp.concatenate([ebuf[:, gy + 1 + dy, pl.ds(8 + gx + dx, 1), :].reshape(8, Z) for dx, dy in around], axis=0)
-    li, lj = iota((Z, Z), 0), iota((Z, Z), 1)
-    after = lj < 64
-    maps = [li == 32 + lj // 8, (li == 31 + (lj + 4) // 8) | (li == 32 + (lj + 4) // 8),
-            li == jnp.where(after, 48, 31), (li == jnp.where(after, 47, 31)) | (li == jnp.where(after, 48, 32))]
-    spread_rows = [lax.dot_general(stacked, m.astype(F32), (((1,), (0,)), ((), ())), precision=HIGH,
-                                   preferred_element_type=F32) for m in maps]
-
-    def cell(kind, vec, y2, dx, dy=0):
-        i = 8 * around.index((dx, dy)) + 2 * vec + y2
-        return wide(spread_rows[kind][i:i + 1])
-
-    def flag(cond):
-        return jnp.where(cond, 1.0, 0.0).astype(F32)
-    x_in, y_in = (flag(gx > 0), flag(gx < nx - 1)), (flag(gy > 0), flag(gy < ny - 1))
-    z_in = jnp.where(lane8 < 64, flag(gz < nz - 1), flag(gz > 0))
-    ends = jnp.where(row8 == 0, zr[0, T2, 0], jnp.where(row8 == 1, zr[1, T2, 0], 0.0))
-    put = (((row8 == 0) & (lane8 >= 64)) | ((row8 == 1) & (lane8 < 64))).astype(F32)
-    third_out = lax.dot_general(ends, put, (((0,), (0,)), ((), ())), precision=HIGH, preferred_element_type=F32)
-    third_out = third_out.reshape(4, 2, Y, Z)
-    for vec in range(4):
-        for dx, others in ((0, (-1, 1)), (-1, (0,)), (1, (0,))):
-            for kind in (0, 2) if dx == 0 else (0,):
-                a = [cell(kind, vec, y2, dx) for y2 in range(2)]
-                mid = a[0] + a[1]
-                y_sum = [jnp.where(row8 < 4, cell(kind, vec, 1, dx, -1) + a[0], mid),
-                         jnp.where(row8 < 4, mid, a[1] + cell(kind, vec, 0, dx, 1))]
-                for h in range(2):
-                    part = slice(8 * h, 8 * h + 8)
-                    base = 0.2 * a[h] + KS * (y_sum[h] + cell(kind + 1, vec, h, dx) + a[h])
-                    for x, other in enumerate(others):
-                        value = base + KS * cell(kind, vec, h, other)
-                        if dx:
-                            side = 0 if dx < 0 else 1
-                            xr[side, C2, vec, part] = xr[side, T2, vec, part] + x_in[side] * value
-                        elif kind == 0:
-                            e2[vec, x, part] = s2[vec, x, part] + value
-                        else:
-                            beyond[vec, x, part] = third_out[vec, x, part] + z_in * value
-        for side, dy, y2 in ((0, -1, 1), (1, 1, 0)):
-            b = cell(0, vec, y2, 0, dy)[0:1]
-            base = 0.2 * b + KS * (2.0 * b + cell(0, vec, 1 - y2, 0)[0:1] + cell(1, vec, y2, 0, dy)[0:1])
-            for x, dx in enumerate((-1, 1)):
-                value = base + KS * cell(0, vec, y2, dx, dy)[0:1]
-                yr[side, C2, vec, x] = yr[side, T2, vec, x] + y_in[side] * value
-
-    corrected(C2, e2, s1, e1, 2, 2)
-    send(C1, e1, 4)
-    receive(C1, e1, 4)
-    corrected(C1, e1, s0, e0, 4, 1)
-    send(C0, e0, 8)
     receive(C0, e0, 8)
     for c in range(4):
         x, near = neighbours(C0, e0, 8, 1, c)
         oper[c:c + 1] = c_fine * (6.0 * x - near)
     for copy, sends in sent:
+        @pl.when(sends)
+        def _():
+            copy.wait_send()
+    for i in range(rounds):
+        sent += [(copy, sends) for copy, sends, _ in chain_copies(i)]
+    for copy, sends in sent[-2 * rounds:]:
         @pl.when(sends)
         def _():
             copy.wait_send()
@@ -558,13 +606,13 @@
             big, big, big, vm(8, 16, 128),
             big, big, big, mid, mid, mid, mid, low, low, low, low, low, mid, vm(4, 16, 128), vm(2, 16, 128), low,
             vm(2, 9, 4, 8, 128), vm(2, 9, 4, 8, 128), vm(2, 10, 4, 16, 128), vm(2, 9, 4, 8, 1, 128),
-            vm(2, 10, 4, 8, 1, 128), vm(2, 9, 4, 1, 128), vm(2, 9, 4, 1, 128),
-            vm(2, 1, 128), vm(2, nx, 1, 128), vm(2, nx, 128), vm(2, 5, ny, nx, 128), vm(1, 128), vm(nz, 1, 128),
+            vm(2, 10, 4, 8, 1, 128), vm(2, 9, 8, 128), vm(2, 9, 8, 128),
+            vm(2, 1, 128), vm(2, nx, 1, 128), vm(2, nx, 128), vm(2, 5, ny, nx, 128), vm(5, 1, 128), vm(2, (nz - 2) // 2, 2, 1, 128), vm(3 * nz, 1, 128),
             vm(2, ny, nx, 128), vm(2, ny, nx, 128), vm(ny, nx, 128), vm(ny, nx, 128), vm(ny // 2, nx, 128),
             vm(8, ny + 2, nx + 16, 128),
             dma((4,)), dma((2, 9)), dma((2, 9)), dma((2, 9)), dma((2, 9)), dma((2, 9)), dma((2, 9)),
             dma((2, nx - 1)), dma((2, nx - 1)), dma((2, 5 * ny - 1)), dma((2, 5 * ny - 1)),
-            dma((nz - 1,)), dma((nz - 1,)),
+            dma((2, (nz - 2) // 2)), dma((2, (nz - 2) // 2)),
         ],
         compiler_params=pltpu.CompilerParams(collective_id=0, has_side_effects=True),
     )(old_basis, previous, incoming, coefficient)

time: 72.2 us -> 67.7 us (0.938)
  Pallas kernels: 71.4 us -> 66.3 us
    pallas_call x1, Pallas kernels: 70.5 us -> 65.4 us  [per_device(): pl.pallas_call(functools.partial(kernel, nx, ny, nz), out_shape=held, in_...]
where the time goes in v3:
time: 67.7 us; the launch traced here: 67 us
  Pallas kernels  66.3 us (98%)
    pallas_call x1, Pallas kernels, per_device(): pl.pallas_call(functools.partial(kernel, nx, ny, nz), out_shape=held, in_...  65.4 us

profile of v3, /device:TPU:1, one launch (start us, length us, event | category | flops | bytes accessed | tf_op | source)
XLA Modules:
  0.0 67.0 jit_solution(5247526761549868933)
XLA Ops:
  0.6 65.4 %shard_map.83 = (f32[4,8,16,128]{3,2,1,0:T(8,128)S(1)}, f32[4,4]{1,0:T(4,128)S(1)}, f32[4,4]{1,0:T(4,128)S(1)}, f32[4,8,16,128]{3,2,1,0:T(8,128)S(1)}, f32[4,8,16,128]{3,2,1,0:T(8,128)S(1)}) custom-call(f32[4,8,16,128]{3,2,1,0:T(8,128)} %old_hbm.1, f32[4,8,16,128]{3,2,1,0:T(8,128)} %prev_hbm.1, f32[4,8,16,128]{3,2,1,0:T(8,128)} %inc_hbm.1, ...), custom_call_target="tpu_custom_call" | custom-call | tf_op jit(solution)/shard_map/pallas_call | solution.py:600
  66.1 0.9 %shard_map.84 = (f32[4,8,16,128]{3,2,1,0:T(8,128)}, f32[4,4]{1,0:T(4,128)}, f32[4,4]{1,0:T(4,128)}, f32[4,8,16,128]{3,2,1,0:T(8,128)}, f32[4,8,16,128]{3,2,1,0:T(8,128)}) custom-call(f32[4,8,16,128]{3,2,1,0:T(8,128)S(1)} %get-tuple-element.10.refs_0_, f32[4,4]{1,0:T(4,128)S(1)} %get-tuple-element.11.refs_1_, f32[4,4]{1,0:T(4,128)S(1)} %get-tuple-element.12.refs_2_, ...), custom_call_target="tpu_custom_call" | custom-call | tf_op jit(solution)/shard_map/pallas_call | solution.py:619

commit v4 on v3

--- a/solution.py
+++ b/solution.py
@@ -42,13 +42,16 @@
 def kernel(nx, ny, nz, old_hbm, prev_hbm, inc_hbm, coef_hbm,
            ortho, proj_ref, tri_ref, e0, oper,
            old, prev, inc, coef,
-           g0, v0, s0, b1, g1, v1, s1, b2, g2, v2, s2, e2, e1, c1, c2, beyond,
+           g0, v0, s0, b1, g1, v1, s1, b2, g2, v2, s2, e2, e1, c1, c2, beyond, h0, h1, h2, exy, ezx, ezy,
            xs, xc, xr, ys, yr, zs, zr, row_s, row_r, line_b, zb, planes, passed, all_planes,
            cc3, inv3, cc4, inv4, inv5, ebuf,
            in_sem, x_send, x_recv, y_send, y_recv, z_send, z_recv,
-           ax_send, ax_recv, az_send, az_recv, ag_send, ag_recv):
+           d_send, d_recv, ax_send, ax_recv, az_send, az_recv, ag_send, ag_recv):
     gx, gy, gz = lax.axis_index("gx"), lax.axis_index("gy"), lax.axis_index("gz")
     X, Y, Z = 8, 16, 128
+
+    def inside_mesh(place, count):
+        return (place >= 0) & (place < count)
 
     def at(dx=0, dy=0, dz=0):
         return (lax.rem(gx + dx + nx, nx), lax.rem(gy + dy + ny, ny), lax.rem(gz + dz + nz, nz))
@@ -148,6 +151,100 @@
                         for i in range(4):
                             xr[side, e, v, pl.ds(i, 4, stride=4), :] = half
 
+    def edges(level, e, n):
+        out = []
+        step = (1, -1)
+        for kind in range(3):
+            for a in range(2):
+                for b in range(2):
+                    i = 2 * a + b
+                    if kind == 0:
+                        src, dst = ys.at[b, e, :, pl.ds((n - 1) if a == 0 else 0, 1)], exy.at[level, i]
+                        d = dict(dx=step[a], dy=step[b])
+                    else:
+                        src, dst = zs.at[b, e], (ezx if kind == 1 else ezy).at[level, i]
+                        d = {"dx" if kind == 1 else "dy": step[a], "dz": step[b]}
+                    full = {"dx": 0, "dy": 0, "dz": 0} | d
+                    sends = receives = None
+                    for key, place, count in (("dx", gx, nx), ("dy", gy, ny), ("dz", gz, nz)):
+                        if full[key]:
+                            to, fro = inside_mesh(place + full[key], count), inside_mesh(place - full[key], count)
+                            sends = to if sends is None else sends & to
+                            receives = fro if receives is None else receives & fro
+                    out.append((copy_to(src, dst, d_send.at[kind, level, i], d_recv.at[kind, level, i], at(**d)),
+                                sends, receives, dst))
+        return out
+
+    def edges_start(level, e, n):
+        for copy, sends, _, _ in edges(level, e, n):
+            sent.append((copy, sends))
+
+            @pl.when(sends)
+            def _():
+                copy.start()
+
+    def edges_clear(level, e, n):
+        for _, _, receives, dst in edges(level, e, n):
+            @pl.when(jnp.logical_not(receives))
+            def _():
+                dst[...] = jnp.zeros(dst.shape, F32)
+
+    def edges_wait(level, e, n):
+        for copy, _, receives, _ in edges(level, e, n):
+            @pl.when(receives)
+            def _():
+                copy.wait_recv()
+
+    def flag(cond):
+        return jnp.where(cond, 1.0, 0.0).astype(F32)
+    x_in, y_in = (flag(gx > 0), flag(gx < nx - 1)), (flag(gy > 0), flag(gy < ny - 1))
+    z_side = (flag(gz > 0), flag(gz < nz - 1))
+
+    def own_part(g, h, n, s):
+        per = 8 // n
+        for c in range(n // 2):
+            part = slice(c * per, (c + 1) * per)
+            x = g[part]
+            row, lane = iota(x.shape, 2), iota(x.shape, 3)
+            near = jnp.where(row >= s, roll(x, s, 2), 0.0) + jnp.where(row < Y - s, roll(x, Y - s, 2), 0.0)
+            near = near + jnp.where(lane >= s, roll(x, s, 3), 0.0) + jnp.where(lane < Z - s, roll(x, Z - s, 3), 0.0)
+            none = jnp.zeros((per, 1, Y, Z), F32)
+            near = near + jnp.concatenate([none, x[:, :-1]], axis=1) + jnp.concatenate([x[:, 1:], none], axis=1)
+            h[part] = 1.2 * x + KS * near
+
+    def complete(level, e_g, e, g, n, s):
+        edges_wait(level, e_g, n)
+        row16, lane16 = iota((Y, Z), 0), iota((Y, Z), 1)
+        lane1 = iota((1, Z), 1)
+        for side in range(2):
+            mine, theirs = (0, n - 1) if side == 0 else (n - 1, 0)
+            for v in range(4):
+                def column(sz):
+                    packed = ezx[level, 2 * side + sz]
+                    k = 2 * n * v + 2 * theirs
+                    return jnp.concatenate([jnp.broadcast_to(packed[:, k + h:k + h + 1], (8, Z)) for h in range(2)], axis=0)
+                add = g[v, mine]
+                add = add + jnp.where(row16 < s, exy[level, 2 * side, v, 0], 0.0)
+                add = add + jnp.where(row16 >= Y - s, exy[level, 2 * side + 1, v, 0], 0.0)
+                add = add + jnp.where(lane16 < s, column(0), 0.0) + jnp.where(lane16 >= Z - s, column(1), 0.0)
+                xr[side, e, v] = xr[side, e, v] + (KS * x_in[side]) * add
+                for x in range(n):
+                    add = g[v, x, 0:1] if side == 0 else g[v, x, Y - 1:Y]
+                    for sx, at_x in ((0, 0), (1, n - 1)):
+                        if x == at_x:
+                            add = add + exy[level, 2 * sx + side, v, 0]
+                    k, r = 2 * n * v + 2 * x + (1 if side == 0 else 0), 7 if side == 0 else 0
+                    lo, hi = (jnp.broadcast_to(ezy[level, 2 * side + sz, r:r + 1, k:k + 1], (1, Z)) for sz in range(2))
+                    add = add + jnp.where(lane1 < s, lo, 0.0) + jnp.where(lane1 >= Z - s, hi, 0.0)
+                    yr[side, e, v, x] = yr[side, e, v, x] + (KS * y_in[side]) * add
+            add = zs[1 - side, e_g]
+            place = lane8 % (2 * n)
+            add = add + jnp.where(place < 2, roll(ezx[level, side], -2 * (n - 1), 1), 0.0)
+            add = add + jnp.where(place >= 2 * n - 2, roll(ezx[level, 2 + side], 2 * (n - 1), 1), 0.0)
+            add = add + jnp.where((row8 < s) & (lane8 % 2 == 0), roll(roll(ezy[level, side], s, 0), -1, 1), 0.0)
+            add = add + jnp.where((row8 >= 8 - s) & (lane8 % 2 == 1), roll(roll(ezy[level, 2 + side], -s, 0), 1, 1), 0.0)
+            zr[side, e] = zr[side, e] + (KS * z_side[side]) * add
+
     def z_halo(e, side, first, count):
         packed = zr[side, e]
         return jnp.concatenate([jnp.broadcast_to(packed[:, i:i + 1], (8, Z)) for i in range(first, first + count)], axis=0)
@@ -187,7 +284,6 @@
             v[c * per:(c + 1) * per] = 1.2 * x + KS * near
 
     def residual(e, b, c_hat, g, v, third, n, s, put):
-        receive(e, v, n)
         per = 8 // n
         for c in range(n // 2):
             part = slice(c * per, (c + 1) * per)
@@ -292,6 +388,15 @@
             out = jnp.where(group == i, roll(zb[k, i], 16 * (i - q), 2), out)
         return out
 
+    for dx in (-1, 1):
+        for dy, dz in ((-1, 0), (1, 0), (0, -1), (0, 1)):
+            reach = (inside_mesh(gx + dx, nx)) & inside_mesh(gy + dy, ny) & inside_mesh(gz + dz, nz)
+            partners = partners + jnp.where(reach, 1, 0)
+
+            @pl.when(reach)
+            def _():
+                pl.semaphore_signal(barrier, inc=1, device_id=at(dx=dx, dy=dy, dz=dz), device_id_type=MESH)
+
     loads[0].wait()
     loads[1].wait()
     c_fine = coef[...]
@@ -300,6 +405,11 @@
         g0[v] = inc[v] * scale
     pl.semaphore_wait(barrier, partners)
     send(G0, g0, 8)
+    edges_start(0, G0, 8)
+    own_part(g0, h0, 8, 1)
+    send(V0, h0, 8)
+    for level, e, n in ((0, G0, 8), (1, G1, 4), (2, G2, 2)):
+        edges_clear(level, e, n)
     for cond, buf, side in ((gx == 0, xr, 0), (gx == nx - 1, xr, 1), (gx == 0, xc, 0), (gx == nx - 1, xc, 1), (gy == 0, yr, 0), (gy == ny - 1, yr, 1),
                             (gz == 0, zr, 0), (gz == nz - 1, zr, 1)):
         @pl.when(cond)
@@ -349,8 +459,8 @@
     start_line(0, to_row(c3.reshape(2, 8, Z)) + gram_row)
 
     second_sweep(G0, g0, v0, 8, 1)
-    send(V0, v0, 8)
-    start_deep(0)
+    receive(V0, h0, 8)
+    complete(0, G0, V0, g0, 8, 1)
 
     def put_b1(part, r):
         b1[part] = r
@@ -358,9 +468,14 @@
     scale1 = (4.0 * KS) / c1[...]
     residual(V0, inc, c_fine, g0, v0, s0, 8, 1, put_b1)
     send(G1, g1, 4)
+    edges_start(1, G1, 4)
+    own_part(g1, h1, 4, 2)
+    send(V1, h1, 4)
+    start_deep(0)
 
     second_sweep(G1, g1, v1, 4, 2)
-    send(V1, v1, 4)
+    receive(V1, h1, 4)
+    complete(1, G1, V1, g1, 4, 2)
     scale2 = (16.0 * KS) / c2[...]
 
     def put_b2(part, r):
@@ -368,18 +483,21 @@
         g2[part] = r * scale2
     residual(V1, b1, 0.25 * c1[...], g1, v1, s1, 4, 2, put_b2)
     send(G2, g2, 2)
+    edges_start(2, G2, 2)
+    own_part(g2, h2, 2, 4)
+    send(V2, h2, 2)
     finish_deep(0)
     for i in range(5):
         planes[i] = jnp.sum(zb[0, i].reshape(ny * nx, Z), axis=0, keepdims=True)
     chain_start(0)
     second_sweep(G2, g2, v2, 2, 4)
-    send(V2, v2, 2)
-    chain_next(1)
+    receive(V2, h2, 2)
+    complete(2, G2, V2, g2, 2, 4)
     held = []
     residual(V2, b2, 0.0625 * c2[...], g2, v2, s2, 2, 4, lambda part, r: held.append(r))
     start_line(1, to_row(held[0].reshape(8, 8, Z)))
     send(T2, s2, 2)
-    chain_next(2)
+    chain_next(1)
 
     shape = (ny, nx, Z)
     lanes = iota(shape, 2)
@@ -403,8 +521,9 @@
 
     start_deep(1)
 
+    chain_next(2)
+    finish_deep(1)
     chain_next(3)
-    finish_deep(1)
     chain_next(4)
 
     rows_i = iota(shape, 1)
@@ -467,9 +586,6 @@
         i = 8 * around.index((dx, dy)) + 2 * vec + y2
         return wide(spread_rows[kind][i:i + 1])
 
-    def flag(cond):
-        return jnp.where(cond, 1.0, 0.0).astype(F32)
-    x_in, y_in = (flag(gx > 0), flag(gx < nx - 1)), (flag(gy > 0), flag(gy < ny - 1))
     z_in = jnp.where(lane8 < 64, flag(gz < nz - 1), flag(gz > 0))
     third_out = jnp.where(iota((128, Z), 1) < 64, z_halo(T2, 1, 0, 16), z_halo(T2, 0, 0, 16)).reshape(4, 2, Y, Z)
     for vec in range(4):
@@ -555,25 +671,22 @@
             for j in range(4):
                 ortho[j, x, part] = sum(inv_w[j][i] * rem[i] for i in range(j + 1))
 
+    for i in range(rounds):
+        sent[:0] = [(copy, sends) for copy, sends, _ in chain_copies(i)]
+    for k in range(2):
+        sent[:0] = [(copy, sends) for copy, sends, _ in deep_copies(k)]
+    for copy, sends in sent[:-6]:
+        @pl.when(sends)
+        def _():
+            copy.wait_send()
     receive(C0, e0, 8)
     for c in range(4):
         x, near = neighbours(C0, e0, 8, 1, c)
         oper[c:c + 1] = c_fine * (6.0 * x - near)
-    for copy, sends in sent:
+    for copy, sends in sent[-6:]:
         @pl.when(sends)
         def _():
             copy.wait_send()
-    for i in range(rounds):
-        sent += [(copy, sends) for copy, sends, _ in chain_copies(i)]
-    for copy, sends in sent[-2 * rounds:]:
-        @pl.when(sends)
-        def _():
-            copy.wait_send()
-    for k in range(2):
-        for copy, sends, _ in deep_copies(k):
-            @pl.when(sends)
-            def _():
-                copy.wait_send()
 
 
 def write_out(*refs):
@@ -605,13 +718,14 @@
         scratch_shapes=[
             big, big, big, vm(8, 16, 128),
             big, big, big, mid, mid, mid, mid, low, low, low, low, low, mid, vm(4, 16, 128), vm(2, 16, 128), low,
+            big, mid, low, vm(3, 4, 4, 1, 1, 128), vm(3, 4, 8, 128), vm(3, 4, 8, 128),
             vm(2, 9, 4, 8, 128), vm(2, 9, 4, 8, 128), vm(2, 10, 4, 16, 128), vm(2, 9, 4, 8, 1, 128),
             vm(2, 10, 4, 8, 1, 128), vm(2, 9, 8, 128), vm(2, 9, 8, 128),
             vm(2, 1, 128), vm(2, nx, 1, 128), vm(2, nx, 128), vm(2, 5, ny, nx, 128), vm(5, 1, 128), vm(2, (nz - 2) // 2, 2, 1, 128), vm(3 * nz, 1, 128),
             vm(2, ny, nx, 128), vm(2, ny, nx, 128), vm(ny, nx, 128), vm(ny, nx, 128), vm(ny // 2, nx, 128),
             vm(8, ny + 2, nx + 16, 128),
             dma((4,)), dma((2, 9)), dma((2, 9)), dma((2, 9)), dma((2, 9)), dma((2, 9)), dma((2, 9)),
-            dma((2, nx - 1)), dma((2, nx - 1)), dma((2, 5 * ny - 1)), dma((2, 5 * ny - 1)),
+            dma((3, 3, 4)), dma((3, 3, 4)), dma((2, nx - 1)), dma((2, nx - 1)), dma((2, 5 * ny - 1)), dma((2, 5 * ny - 1)),
             dma((2, (nz - 2) // 2)), dma((2, (nz - 2) // 2)),
         ],
         compiler_params=pltpu.CompilerParams(collective_id=0, has_side_effects=True),

time: 67.7 us -> 65.1 us (0.962)
  Pallas kernels: 66.3 us -> 64.3 us
    pallas_call x1, Pallas kernels: 65.4 us -> 63.3 us  [per_device(): pl.pallas_call(functools.partial(kernel, nx, ny, nz), out_shape=held, in_...]
where the time goes in v4:
time: 65.1 us; the launch traced here: 64.9 us
  Pallas kernels  64.3 us (99%)
    pallas_call x1, Pallas kernels, per_device(): pl.pallas_call(functools.partial(kernel, nx, ny, nz), out_shape=held, in_...  63.3 us

profile of v4, /device:TPU:1, one launch (start us, length us, event | category | flops | bytes accessed | tf_op | source)
XLA Modules:
  0.0 64.9 jit_solution(17381939292895134303)
XLA Ops:
  0.6 63.3 %shard_map.83 = (f32[4,8,16,128]{3,2,1,0:T(8,128)S(1)}, f32[4,4]{1,0:T(4,128)S(1)}, f32[4,4]{1,0:T(4,128)S(1)}, f32[4,8,16,128]{3,2,1,0:T(8,128)S(1)}, f32[4,8,16,128]{3,2,1,0:T(8,128)S(1)}) custom-call(f32[4,8,16,128]{3,2,1,0:T(8,128)} %old_hbm.1, f32[4,8,16,128]{3,2,1,0:T(8,128)} %prev_hbm.1, f32[4,8,16,128]{3,2,1,0:T(8,128)} %inc_hbm.1, ...), custom_call_target="tpu_custom_call" | custom-call | tf_op jit(solution)/shard_map/pallas_call | solution.py:713
  64.0 0.9 %shard_map.84 = (f32[4,8,16,128]{3,2,1,0:T(8,128)}, f32[4,4]{1,0:T(4,128)}, f32[4,4]{1,0:T(4,128)}, f32[4,8,16,128]{3,2,1,0:T(8,128)}, f32[4,8,16,128]{3,2,1,0:T(8,128)}) custom-call(f32[4,8,16,128]{3,2,1,0:T(8,128)S(1)} %get-tuple-element.10.refs_0_, f32[4,4]{1,0:T(4,128)S(1)} %get-tuple-element.11.refs_1_, f32[4,4]{1,0:T(4,128)S(1)} %get-tuple-element.12.refs_2_, ...), custom_call_target="tpu_custom_call" | custom-call | tf_op jit(solution)/shard_map/pallas_call | solution.py:733
